TPU v7x, 256 devices: a whole 4x4x8 slice. The times are simulated.
256 devices in a mesh: loop: 4 (over x_lo, core), sub: 64 (over z, y, x_hi).
Axes of the slice: x: 4 (x_hi: 2, x_lo: 2; x = x_hi * 2 + x_lo), y: 4, z: 8, core: 2. Of those that a mesh axis runs over, the one named last changes fastest.
Arguments:
- rate: float32 [8192, 5, 384], P(('loop', 'sub')), may hold values from 0 to 1
- phase: float32 [8192, 5, 384], P(('loop', 'sub')), may hold values from -3.140625 to 3.140625
- forcing: float32 [2, 4, 8192, 5, 384], P(None, None, ('loop', 'sub')), may hold values from -8 to 8
Outputs:
- response: float32 [2, 4, 8192, 5, 384], P(None, None, ('loop', 'sub'))
All inputs are finite; a program needn't handle non-finite values.
Results may differ from a plain program's by a relative error of at most 0.0003.
Values sent between devices are 32-bit elements; how exact they have to be, the bound alone decides.
A program may use at most 128 MiB of HBM per device.

v0:
```python
import jax
import jax.numpy as jnp
from jax import lax
from jax.sharding import PartitionSpec as P

fringe_total = 0.7


def carried_in(value, axis, join, neutral):
    count, mine = (lax.axis_size(axis), lax.axis_index(axis))
    pieces = jax.tree.map(lambda part: lax.all_gather(part, axis), value)
    subtotal = jax.tree.map(
        lambda part, zero: jnp.full_like(part, 0) + jnp.asarray(zero, part.dtype), value, neutral
    )

    def hop(position, subtotal):
        longer = join(subtotal, jax.tree.map(lambda part: part[position], pieces))
        return jax.tree.map(lambda new, old: jnp.where(position < mine, new, old), longer, subtotal)

    return lax.fori_loop(0, count - 1, hop, subtotal)


def broadcast(value, axis, source):
    kept = jnp.where(lax.axis_index(axis) == source, value, 0).astype(value.dtype)
    return lax.psum(kept, axis)


def complex_product(left, right):
    return jnp.stack(
        [left[0] * right[0] - left[1] * right[1], left[0] * right[1] + left[1] * right[0]]
    )


def compose(earlier, later):
    return (complex_product(later[0], earlier[0]), complex_product(later[0], earlier[1]) + later[1])


def local(rate, phase, forcing):
    stations = rate.shape[0]
    devices = lax.axis_size(("loop", "sub"))
    is_last = lax.axis_index(("loop", "sub")) == devices - 1
    fringe_sponge = jnp.where(
        is_last, jnp.float32(fringe_total ** (1.0 / stations)), jnp.float32(1.0)
    )
    magnitude = jnp.exp(-rate) * fringe_sponge
    coeff = jnp.stack([magnitude * jnp.cos(phase), magnitude * jnp.sin(phase)])[:, None]
    source = jnp.sqrt(-jnp.expm1(-2.0 * rate)) * forcing
    local_a, local_b = lax.associative_scan(compose, (coeff, source), axis=2)
    own = (local_a[:, :, -1], local_b[:, :, -1])
    unit = (
        jnp.stack([jnp.ones_like(own[0][0]), jnp.zeros_like(own[0][0])]),
        jnp.zeros_like(own[1]),
    )
    before = carried_in((own[0], own[1]), ("loop", "sub"), compose, unit)
    through = compose(before, own)
    circuit_transfer = (
        broadcast(through[0], ("loop", "sub"), devices - 1),
        broadcast(through[1], ("loop", "sub"), devices - 1),
    )
    denom_re = 1.0 - circuit_transfer[0][0]
    denom_im = -circuit_transfer[0][1]
    scale = denom_re * denom_re + denom_im * denom_im
    closing = complex_product(circuit_transfer[1], jnp.stack([denom_re, -denom_im])) / scale
    entering = complex_product(before[0], closing) + before[1]
    return local_b + complex_product(local_a, entering[:, :, None])


def solution(mesh):
    placed = (
        P(("loop", "sub"), None, None),
        P(("loop", "sub"), None, None),
        P(None, None, ("loop", "sub"), None, None),
    )
    return jax.shard_map(
        local,
        mesh=mesh,
        in_specs=placed,
        out_specs=P(None, None, ("loop", "sub"), None, None),
        check_vma=False,
    )
```

profile of v0, /device:TPU:1, one launch (start us, length us, event | category | flops | bytes accessed | tf_op | source)
XLA Modules:
  0.0 2151.6 jit_solution(167800945347909830)
XLA Ops:
  6.5 2.1 multiply_bitcast_fusion.1
  14.3 2.9 copy_multiply_fusion
  22.9 7.1 pad.65
  31.4 14.1 pad.67
  46.3 1.1 multiply_subtract_fusion.9
  47.4 1.0 maximum_add_fusion.7
  49.2 18.9 pad.66
  68.1 2.0 add.312
  70.0 1.3 multiply_subtract_fusion.5
  72.4 28.2 %pad.68 = f32[2,4,16,5,384]{4,1,3,2,0:T(4,128)S(1)} pad(f32[2,4,8,5,384]{4,1,3,2,0:T(4,128)} %pad_maximum_fusion.1, f32[]{:T(128)} %constant.47.clone.1), padding=0_0_0x0_0_0x0_1_1x0_0_0x0_0_0 | pad | bytes 1474564 | tf_op jit(solution)/shard_map/pad | solution.py:48
  100.6 25.2 %pad.69 = f32[2,4,16,5,384]{4,1,3,2,0:T(4,128)} pad(f32[2,4,8,5,384]{4,1,3,2,0:T(4,128)S(1)} %copy-done.7, f32[]{:T(128)} %constant.47.clone.1), padding=0_0_0x0_0_0x1_0_1x0_0_0x0_0_0 | pad | bytes 1474564 | tf_op jit(solution)/shard_map/pad | solution.py:48
  125.8 2.4 add.315
  128.2 71.2 %pad.71 = f32[2,4,32,5,384]{4,1,3,2,0:T(4,128)} pad(f32[2,4,16,5,384]{4,1,3,2,0:T(4,128)} %add.315, f32[]{:T(128)} %constant.47.clone.1), padding=0_0_0x0_0_0x1_0_1x0_0_0x0_0_0 | pad | bytes 2949124 | tf_op jit(solution)/shard_map/pad | solution.py:48
  199.5 1.5 multiply_subtract_fusion.3
  202.1 49.6 %pad.70 = f32[2,4,32,5,384]{4,1,3,2,0:T(4,128)} pad(f32[2,4,16,5,384]{4,1,3,2,0:T(4,128)S(1)} %pad_maximum_fusion, f32[]{:T(128)} %constant.47.clone.1), padding=0_0_0x0_0_0x0_1_1x0_0_0x0_0_0 | pad | bytes 2949124 | tf_op jit(solution)/shard_map/pad | solution.py:48
  251.7 1.5 slice_add_fusion.8
  253.5 1.8 add_bitcast_fusion
  255.3 469.6 %all-gather.5.cloned.1.call-done = f32[512,1,1,5,384]{4,2,3,1,0:T(1,128)} async-done(((f32[2,1,1,5,384]{4,2,3,1,0:T(1,128)}), f32[512,1,1,5,384]{4,2,3,1,0:T(1,128)}) %all-gather.5.cloned.1.call-update) | async-done | bytes 3932176 | tf_op jit(solution)/shard_map/all_gather | solution.py:11
  724.9 731.3 %all-gather.7.cloned.1.call-done = f32[512,4,1,5,384]{4,1,3,2,0:T(4,128)} async-done(((f32[2,4,1,5,384]{4,1,3,2,0:T(4,128)}), f32[512,4,1,5,384]{4,1,3,2,0:T(4,128)}) %all-gather.7.cloned.1.call-update) | async-done | bytes 15728656 | tf_op jit(solution)/shard_map/all_gather | solution.py:11
  1456.2 440.8 %while.16 = (s32[]{:T(128)}, f32[2,1,5,384]{3,2,1,0:T(8,128)S(1)}, f32[2,4,5,384]{3,2,1,0:T(8,128)S(1)}, s32[]{:T(128)}, f32[256,2,1,5,384]{4,2,3,1,0:T(1,128)},...) while((s32[]{:T(128)}, f32[2,1,5,384]{3,2,1,0:T(8,128)S(1)}, ...), condition=%wide.region_1.2_spmd.clone, body=%wide.region_0.1_spmd.clone.sunk | while | flops 142085 | bytes 783507 | solution.py:20
  1897.0 0.9 fusion.14
  1899.5 1.1 copy.107
  1900.7 239.8 %all-reduce.23.cloned.1.call-done = (f32[2,4,5,384]{3,1,2,0:T(4,128)}, f32[2,1,5,384]{3,0,2,1:T(2,128)}) async-done(((f32[2,4,5,384]{3,1,2,0:T(4,128)}, f32[2,1,5,384]{3,0,2,1:T(2,128)}), (f32[2,4,5,384]{3,1,2,0:T(4,128)}, f32[2,1,5,384]{3,0,2,1:T(2,128)})) %all-reduce.23.cloned.1.call-update) | async-done | bytes 76816 | tf_op jit(solution)/shard_map/psum | solution.py:25
  2143.6 1.5 copy.117
  (2191 shorter events, 446.0 us)
Async XLA Ops:
  6.5 718.4 %all-gather.5.cloned.1.call-start = ((), (), s32[]{:S(2)}) async-start(), calls=%async_computation | async-start | bytes 3947520 | tf_op jit(solution)/shard_map/all_gather | solution.py:11
  12.3 1.8 copy-start.4
  13.3 0.8 copy-start.6
  14.0 1442.2 %all-gather.7.cloned.1.call-start = ((), (), s32[]{:S(2)}) async-start(), calls=%async_computation.1 | async-start | bytes 15790080 | tf_op jit(solution)/shard_map/all_gather | solution.py:11
  18.6 3.2 copy-start.3
  21.8 26.6 %slice-start = ((f32[2,4,8,5,384]{4,1,3,2,0:T(4,128)}), f32[2,4,1,5,384]{4,1,3,2,0:T(4,128)S(1)}, s32[]{:S(2)}) async-start(f32[2,4,8,5,384]{4,1,3,2,0:T(4,128)} %copy-done.3), calls=%async_computation.3 | async-start | bytes 122880 | tf_op jit(solution)/shard_map/slice | solution.py:48
  22.2 7.8 copy-start.8
  30.0 0.7 copy-start.9
  68.1 3.4 copy-start.14
  71.3 29.3 %copy-start.7 = (f32[2,4,8,5,384]{4,1,3,2,0:T(4,128)S(1)}, f32[2,4,8,5,384]{4,1,3,2,0:T(4,128)}, u32[]{:S(2)}) copy-start(f32[2,4,8,5,384]{4,1,3,2,0:T(4,128)} %add.312) | copy-start | bytes 1474564
  128.2 71.2 %copy-start.12 = (f32[15,5,384]{2,0,1:T(8,128)S(1)}, f32[15,5,384]{2,0,1:T(8,128)}, u32[]{:S(2)}) copy-start(f32[15,5,384]{2,0,1:T(8,128)} %get-tuple-element.213) | copy-start | bytes 345604
  128.2 71.2 %copy-start.11 = (f32[15,5,384]{2,0,1:T(8,128)S(1)}, f32[15,5,384]{2,0,1:T(8,128)}, u32[]{:S(2)}) copy-start(f32[15,5,384]{2,0,1:T(8,128)} %get-tuple-element.212) | copy-start | bytes 345604
  201.0 0.8 copy-start.13
  202.1 49.6 %copy-start = (f32[2,4,32,5,384]{4,1,3,2,0:T(4,128)S(1)}, f32[2,4,32,5,384]{4,1,3,2,0:T(4,128)}, u32[]{:S(2)}) copy-start(f32[2,4,32,5,384]{4,1,3,2,0:T(4,128)} %pad.71) | copy-start | bytes 5898244
  202.1 51.4 %copy-start.5 = (f32[2,1,32,5,384]{4,2,3,1,0:T(8,128)S(1)}, f32[2,1,32,5,384]{4,2,3,1,0:T(8,128)}, u32[]{:S(2)}) copy-start(f32[2,1,32,5,384]{4,2,3,1,0:T(8,128)} %copy-done.4) | copy-start | bytes 1474564
  202.1 1254.1 %copy-start.2 = (f32[2,1,5,384]{3,2,1,0:T(8,128)S(1)}, f32[2,1,5,384]{3,2,1,0:T(8,128)}, u32[]{:S(2)}) copy-start(f32[2,1,5,384]{3,2,1,0:T(8,128)} %constant.49.clone.1) | copy-start | bytes 46084
  253.2 1887.2 %all-reduce.23.cloned.1.call-start = ((), (), s32[]{:S(2)}) async-start(), calls=%async_computation.2 | async-start | bytes 153600 | tf_op jit(solution)/shard_map/psum | solution.py:25
  1456.2 441.8 %copy-start.10 = (f32[2,4,1,5,384]{4,1,3,2,0:T(4,128)S(1)}, f32[2,4,1,5,384]{4,1,3,2,0:T(4,128)}, u32[]{:S(2)}) copy-start(f32[2,4,1,5,384]{4,1,3,2,0:T(4,128)} %slice_add_fusion.8) | copy-start | bytes 184324
  2140.5 2.2 copy-start.1
Sparse Core Ops, SparseCore 0:
  14.1 710.7 all-gather.4
  726.8 729.3 all-gather.6
  1899.5 240.9 all-reduce.22
where the time goes:
time: 2180 us; the launch traced here: 2150 us
  waiting for transfers between devices  1440 us (66%)
  local copies, waits for them, and re-layouts  627 us (29%)
  other arithmetic  54.5 us (2%)
    all_gather x2, waiting for transfers between devices, carried_in(): pieces = jax.tree.map(lambda part: lax.all_gather(part, axis), value)  1200 us
    psum x1, waiting for transfers between devices, broadcast(): return lax.psum(kept, axis)  240 us
    pad x16, local copies, waits for them, and re-layouts, local(): local_a, local_b = lax.associative_scan(compose, (coeff, source), axis=2)  216 us
    dynamic_slice x255, local copies, waits for them, and re-layouts, hop(): longer = join(subtotal, jax.tree.map(lambda part: part[position], pieces))  215 us
    slice x255, local copies, waits for them, and re-layouts, complex_product(): left[1] * right[1]  185 us
  transfers between devices with their start and end apart: 3, of which 3 were waited for; matrix products, arithmetic and copies ran while one was open for 11% of the time, Pallas kernels for 0%

commit v1 on v0

v1 whole, which is shorter than its diff:
```python
import functools

import jax
import jax.numpy as jnp
from jax import lax
from jax.experimental import pallas as pl
from jax.experimental.pallas import tpu as pltpu
from jax.sharding import PartitionSpec as P

fringe_total = 0.7
FRINGE_STATIONS = 32
AXES = ("loop", "sub")


def map_kernel(coef_ref, scale_ref, f_ref, out_ref):
    stations = scale_ref.shape[0]
    ex = f_ref.shape[1]

    def step(i, carry):
        pr, pi, xr, xi = carry
        cr = coef_ref[0, i]
        ci = coef_ref[1, i]
        sc = scale_ref[i]
        npr = cr * pr - ci * pi
        npi = cr * pi + ci * pr
        nxr, nxi = [], []
        for e in range(ex):
            nxr.append(cr * xr[e] - ci * xi[e] + sc * f_ref[0, e, i])
            nxi.append(cr * xi[e] + ci * xr[e] + sc * f_ref[1, e, i])
        return npr, npi, tuple(nxr), tuple(nxi)

    shape = scale_ref.shape[1:]
    one = jnp.ones(shape, jnp.float32)
    zero = jnp.zeros(shape, jnp.float32)
    init = (one, zero, (zero,) * ex, (zero,) * ex)
    pr, pi, xr, xi = lax.fori_loop(0, stations, step, init, unroll=8)
    for e in range(ex):
        out_ref[0, e] = xr[e]
        out_ref[1, e] = xi[e]
    out_ref[0, ex] = pr
    out_ref[1, ex] = pi


def march_kernel(coef_ref, scale_ref, f_ref, x0_ref, out_ref):
    stations = scale_ref.shape[0]
    ex = f_ref.shape[1]

    def step(i, carry):
        xr, xi = carry
        cr = coef_ref[0, i]
        ci = coef_ref[1, i]
        sc = scale_ref[i]
        nxr, nxi = [], []
        for e in range(ex):
            r = cr * xr[e] - ci * xi[e] + sc * f_ref[0, e, i]
            m = cr * xi[e] + ci * xr[e] + sc * f_ref[1, e, i]
            out_ref[0, e, i] = r
            out_ref[1, e, i] = m
            nxr.append(r)
            nxi.append(m)
        return tuple(nxr), tuple(nxi)

    init = (tuple(x0_ref[0, e] for e in range(ex)), tuple(x0_ref[1, e] for e in range(ex)))
    lax.fori_loop(0, stations, step, init, unroll=8)


def vmem_call(kernel, out_shape, n_in):
    return pl.pallas_call(
        kernel,
        out_shape=out_shape,
        in_specs=[pl.BlockSpec(memory_space=pltpu.VMEM)] * n_in,
        out_specs=pl.BlockSpec(memory_space=pltpu.VMEM),
    )


def compose(earlier, later):
    ex = earlier.shape[1] - 1
    ar, ai = later[0, ex:], later[1, ex:]
    br, bi = earlier[0], earlier[1]
    nr = ar * br - ai * bi
    ni = ar * bi + ai * br
    offset = jnp.stack([nr[:ex], ni[:ex]]) + later[:, :ex]
    gain = jnp.stack([nr[ex:], ni[ex:]])
    return jnp.concatenate([offset, gain], axis=1)


def shift(value, distance, count):
    return lax.ppermute(value, AXES, [(i, (i + distance) % count) for i in range(count)])


def local(rate, phase, forcing):
    stations, fields, wall = rate.shape
    ex = forcing.shape[1]
    count = lax.axis_size(AXES)
    total = stations * count
    me = lax.axis_index(AXES)
    index = me * stations + jnp.arange(stations)
    sponge = jnp.where(
        index >= total - FRINGE_STATIONS,
        jnp.float32(fringe_total ** (1.0 / FRINGE_STATIONS)),
        jnp.float32(1.0),
    )
    magnitude = jnp.exp(-rate) * sponge[:, None, None]
    coef = jnp.stack([magnitude * jnp.cos(phase), magnitude * jnp.sin(phase)])
    scale = jnp.sqrt(-jnp.expm1(-2.0 * rate))

    own = vmem_call(
        map_kernel, jax.ShapeDtypeStruct((2, ex + 1, fields, wall), jnp.float32), 3
    )(coef, scale, forcing)

    loop_map = shift(own, 1, count)
    reach = 1
    while reach < count:
        loop_map = compose(shift(loop_map, reach, count), loop_map)
        reach *= 2

    gr, gi = loop_map[0, ex], loop_map[1, ex]
    denom_re = 1.0 - gr
    denom_im = -gi
    size = denom_re * denom_re + denom_im * denom_im
    br, bi = loop_map[0, :ex], loop_map[1, :ex]
    entering = jnp.stack(
        [(br * denom_re + bi * denom_im) / size, (bi * denom_re - br * denom_im) / size]
    )

    return vmem_call(
        march_kernel, jax.ShapeDtypeStruct(forcing.shape, jnp.float32), 4
    )(coef, scale, forcing, entering)


def solution(mesh):
    count = mesh.shape["loop"] * mesh.shape["sub"]
    assert count & (count - 1) == 0
    placed = (
        P(AXES, None, None),
        P(AXES, None, None),
        P(None, None, AXES, None, None),
    )
    return jax.shard_map(
        local,
        mesh=mesh,
        in_specs=placed,
        out_specs=P(None, None, AXES, None, None),
        check_vma=False,
    )
```

time: 2180 us -> 100 us (0.05); the launches traced: 2150 us -> 99.2 us
  waiting for transfers between devices: 1440 us -> 68.4 us
  local copies, waits for them, and re-layouts: 627 us -> 8 us
  other arithmetic: 54.5 us -> 6.78 us
    all_gather x2 -> x0, waiting for transfers between devices: 1200 us -> none  [carried_in(): pieces = jax.tree.map(lambda part: lax.all_gather(part, axis), value)]
    psum x1 -> x0, waiting for transfers between devices: 240 us -> none  [broadcast(): return lax.psum(kept, axis)]
    pad x16 -> x0, local copies, waits for them, and re-layouts: 216 us -> none  [local(): local_a, local_b = lax.associative_scan(compose, (coeff, source), axis=2)]
    dynamic_slice x255 -> x0, local copies, waits for them, and re-layouts: 215 us -> none  [hop(): longer = join(subtotal, jax.tree.map(lambda part: part[position], pieces))]
    slice x275 -> x0, local copies, waits for them, and re-layouts: 188 us -> none  [the longest x255 185 us: complex_product(): left[1] * right[1]]
    ppermute x0 -> x9, waiting for transfers between devices: none -> 68.4 us  [shift(): lax.ppermute(value, AXES, [(i, (i + distance) % count) for i in range(cou...]
  transfers between devices with their start and end apart: 3 -> 9, of which waited for: 3 -> 9; matrix products, arithmetic and copies ran while one was open for 11% -> 0% of each run, Pallas kernels for 0% -> 0%
where the time goes in v1:
time: 100 us; the launch traced here: 99.2 us
  waiting for transfers between devices  68.4 us (68%)
  local copies, waits for them, and re-layouts  8 us (8%)
  Pallas kernels  7.99 us (8%)
  starting transfers between devices  7.64 us (8%)
  other arithmetic  6.78 us (7%)
    ppermute x9, waiting for transfers between devices, shift(): lax.ppermute(value, AXES, [(i, (i + distance) % count) for i in range(cou...  68.4 us
    ppermute x9, starting transfers between devices, shift(): lax.ppermute(value, AXES, [(i, (i + distance) % count) for i in range(cou...  7.64 us
    pallas_call x1, Pallas kernels, local(): vmem_call(march_kernel, jax.ShapeDtypeStruct(forcing.shape, jnp.float32), 4)  4.48 us
    unnamed x3, local copies, waits for them, and re-layouts  4.34 us
    pallas_call x1, Pallas kernels, local(): vmem_call(map_kernel, jax.ShapeDtypeStruct((2, ex + 1, fields, wall), jnp...  3.52 us
    pallas_call x1, local copies, waits for them, and re-layouts, local(): vmem_call(march_kernel, jax.ShapeDtypeStruct(forcing.shape, jnp.float32), 4)  3.51 us
    another operation x2, other arithmetic, local(): coef = jnp.stack([magnitude * jnp.cos(phase), magnitude * jnp.sin(phase)])  2.49 us
  transfers between devices with their start and end apart: 9, of which 9 were waited for; matrix products, arithmetic and copies ran while one was open for 0% of the time, Pallas kernels for 0%

profile of v1, /device:TPU:1, one launch (start us, length us, event | category | flops | bytes accessed | tf_op | source)
XLA Modules:
  0.0 99.2 jit_solution(7184353641520408158)
XLA Ops:
  0.0 1.0 %neg.10 = f32[32,5,384]{2,0,1:T(8,128)S(1)} negate(f32[32,5,384]{2,0,1:T(8,128)} %param.3) | non-fusion elementwise | flops 61440 | bytes 491520 | tf_op jit(solution)/shard_map/neg | solution.py:103
  1.0 2.0 %fusion.6.scale_ref = f32[32,5,384]{2,1,0:T(8,128)} fusion(f32[32,5,384]{2,0,1:T(8,128)} %param.3), kind=kLoop, calls=%fused_computation.10 | loop fusion | flops 122880 | bytes 491520 | tf_op jit(solution)/shard_map/sqrt | solution.py:105
  3.0 4.3 %copy.16.f_ref = f32[2,4,32,5,384]{4,3,2,1,0:T(8,128)} copy(f32[2,4,32,5,384]{4,2,3,1,0:T(8,128)} %param.5) | data formatting | bytes 3932160 | tf_op args[2]
  7.3 1.5 %fusion.1 = (f32[1,32,5,384]{3,2,1,0:T(8,128)S(1)}, f32[1,32,5,384]{3,2,1,0:T(8,128)S(1)}) fusion(f32[32,5,384]{2,0,1:T(8,128)S(1)} %copy-done, f32[32,5,384]{2,0,1:T(8,128)S(1)} %neg.10, f32[32]{0:T(128)S(1)} %compare_select_fusion), kind=kLoop, calls=%fused_computation.4 | loop fusion | flops 184320 | bytes 983168 | tf_op jit(solution)/shard_map/stack | solution.py:104
  8.9 1.0 pad_maximum_fusion.coef_ref
  9.8 3.5 %shard_map.37 = f32[2,5,5,384]{3,2,1,0:T(8,128)} custom-call(f32[2,32,5,384]{3,2,1,0:T(8,128)} %pad_maximum_fusion.coef_ref, f32[32,5,384]{2,1,0:T(8,128)} %fusion.6.scale_ref, f32[2,4,32,5,384]{4,3,2,1,0:T(8,128)} %copy.16.f_ref), custom_call_target="tpu_custom_call" | custom-call | tf_op jit(solution)/shard_map/pallas_call | solution.py:107
  13.4 3.6 %collective-permute-start = (f32[2,5,5,384]{3,2,1,0:T(8,128)}, f32[2,5,5,384]{3,2,1,0:T(8,128)S(1)}, u32[]{:S(2)}, u32[]{:S(2)}) collective-permute-start(f32[2,5,5,384]{3,2,1,0:T(8,128)} %shard_map.37), channel_id=1, source_target_pairs={{0,1},{1,2},{2,3},{3,4},{4,5},{5,6},{6,7},{7,8},{8,9},{9,10},{10,1... | collective-permute-start | bytes 230408 | tf_op jit(solution)/shard_map/ppermute | solution.py:88
  16.9 11.5 %collective-permute-done = f32[2,5,5,384]{3,2,1,0:T(8,128)S(1)} collective-permute-done((f32[2,5,5,384]{3,2,1,0:T(8,128)}, f32[2,5,5,384]{3,2,1,0:T(8,128)S(1)}, u32[]{:S(2)}, u32[]{:S(2)}) %collective-permute-start) | collective-permute-done | bytes 76832 | tf_op jit(solution)/shard_map/ppermute | solution.py:88
  28.5 10.1 %collective-permute-done.1 = f32[2,5,5,384]{3,2,1,0:T(8,128)S(1)} collective-permute-done((f32[2,5,5,384]{3,2,1,0:T(8,128)S(1)}, f32[2,5,5,384]{3,2,1,0:T(8,128)S(1)}, u32[]{:S(2)}, u32[]{:S(2)}) %collective-permute-start.1) | collective-permute-done | bytes 76832 | tf_op jit(solution)/shard_map/ppermute | solution.py:88
  38.8 8.3 %collective-permute-done.2 = f32[2,5,5,384]{3,2,1,0:T(8,128)S(1)} collective-permute-done((f32[2,5,5,384]{3,2,1,0:T(8,128)S(1)}, f32[2,5,5,384]{3,2,1,0:T(8,128)S(1)}, u32[]{:S(2)}, u32[]{:S(2)}) %collective-permute-start.2) | collective-permute-done | bytes 76832 | tf_op jit(solution)/shard_map/ppermute | solution.py:88
  47.2 0.1 collective-permute-start.3
  47.3 8.7 %collective-permute-done.3 = f32[2,5,5,384]{3,2,1,0:T(8,128)S(1)} collective-permute-done((f32[2,5,5,384]{3,2,1,0:T(8,128)S(1)}, f32[2,5,5,384]{3,2,1,0:T(8,128)S(1)}, u32[]{:S(2)}, u32[]{:S(2)}) %collective-permute-start.3) | collective-permute-done | bytes 76832 | tf_op jit(solution)/shard_map/ppermute | solution.py:88
  56.1 0.1 collective-permute-start.4
  56.2 5.5 %collective-permute-done.4 = f32[2,5,5,384]{3,2,1,0:T(8,128)S(1)} collective-permute-done((f32[2,5,5,384]{3,2,1,0:T(8,128)S(1)}, f32[2,5,5,384]{3,2,1,0:T(8,128)S(1)}, u32[]{:S(2)}, u32[]{:S(2)}) %collective-permute-start.4) | collective-permute-done | bytes 76832 | tf_op jit(solution)/shard_map/ppermute | solution.py:88
  61.9 0.1 collective-permute-start.5
  62.0 6.4 %collective-permute-done.5 = f32[2,5,5,384]{3,2,1,0:T(8,128)S(1)} collective-permute-done((f32[2,5,5,384]{3,2,1,0:T(8,128)S(1)}, f32[2,5,5,384]{3,2,1,0:T(8,128)S(1)}, u32[]{:S(2)}, u32[]{:S(2)}) %collective-permute-start.5) | collective-permute-done | bytes 76832 | tf_op jit(solution)/shard_map/ppermute | solution.py:88
  68.6 13.1 %collective-permute-done.6 = f32[2,5,5,384]{3,2,1,0:T(8,128)S(1)} collective-permute-done((f32[2,5,5,384]{3,2,1,0:T(8,128)S(1)}, f32[2,5,5,384]{3,2,1,0:T(8,128)S(1)}, u32[]{:S(2)}, u32[]{:S(2)}) %collective-permute-start.6) | collective-permute-done | bytes 76832 | tf_op jit(solution)/shard_map/ppermute | solution.py:88
  81.9 1.1 %collective-permute-start.7 = (f32[2,5,5,384]{3,2,1,0:T(8,128)S(1)}, f32[2,5,5,384]{3,2,1,0:T(8,128)S(1)}, u32[]{:S(2)}, u32[]{:S(2)}) collective-permute-start(f32[2,5,5,384]{3,2,1,0:T(8,128)S(1)} %maximum_maximum_fusion.5), channel_id=1, source_target_pairs={{0,64},{1,65},{2,66},{3,67},{4,68},{5,69},{6,70},{7,71},{8,72},{9,... | collective-permute-start | bytes 230408 | tf_op jit(solution)/shard_map/ppermute | solution.py:88
  83.0 2.5 %collective-permute-done.7 = f32[2,5,5,384]{3,2,1,0:T(8,128)S(1)} collective-permute-done((f32[2,5,5,384]{3,2,1,0:T(8,128)S(1)}, f32[2,5,5,384]{3,2,1,0:T(8,128)S(1)}, u32[]{:S(2)}, u32[]{:S(2)}) %collective-permute-start.7) | collective-permute-done | bytes 76832 | tf_op jit(solution)/shard_map/ppermute | solution.py:88
  85.7 2.5 %collective-permute-start.8 = (f32[2,5,5,384]{3,2,1,0:T(8,128)S(1)}, f32[2,5,5,384]{3,2,1,0:T(8,128)S(1)}, u32[]{:S(2)}, u32[]{:S(2)}) collective-permute-start(f32[2,5,5,384]{3,2,1,0:T(8,128)S(1)} %maximum_maximum_fusion.6), channel_id=1, source_target_pairs={{0,128},{1,129},{2,130},{3,131},{4,132},{5,133},{6,134},{7,135},{8... | collective-permute-start | bytes 230408 | tf_op jit(solution)/shard_map/ppermute | solution.py:88
  88.2 2.3 %collective-permute-done.8 = f32[2,5,5,384]{3,2,1,0:T(8,128)S(1)} collective-permute-done((f32[2,5,5,384]{3,2,1,0:T(8,128)S(1)}, f32[2,5,5,384]{3,2,1,0:T(8,128)S(1)}, u32[]{:S(2)}, u32[]{:S(2)}) %collective-permute-start.8) | collective-permute-done | bytes 76832 | tf_op jit(solution)/shard_map/ppermute | solution.py:88
  90.6 0.6 pad_maximum_fusion.1.x0_ref
  91.3 4.5 %shard_map.38 = f32[2,4,32,5,384]{4,3,2,1,0:T(8,128)} custom-call(f32[2,32,5,384]{3,2,1,0:T(8,128)} %pad_maximum_fusion.coef_ref, f32[32,5,384]{2,1,0:T(8,128)} %fusion.6.scale_ref, f32[2,4,32,5,384]{4,3,2,1,0:T(8,128)} %copy.16.f_ref, f32[2,4,5,384]{3,2,1,0:T(8,128)} %pad_maximum_fusion.1.x0_ref), custom_call_target="tpu_custom_call" | custom-call | tf_op jit(solution)/shard_map/pallas_call | solution.py:126
  95.7 3.5 %copy.17 = f32[2,4,32,5,384]{4,2,3,1,0:T(8,128)} copy(f32[2,4,32,5,384]{4,3,2,1,0:T(8,128)} %shard_map.38) | data formatting | bytes 3932160 | tf_op jit(solution)/shard_map/pallas_call | solution.py:126
  (60 shorter events, 1.0 us)
Async XLA Ops:
  0.0 7.3 %copy-start = (f32[32,5,384]{2,0,1:T(8,128)S(1)}, f32[32,5,384]{2,0,1:T(8,128)}, u32[]{:S(2)}) copy-start(f32[32,5,384]{2,0,1:T(8,128)} %param.4) | copy-start | bytes 737284
  13.4 15.1 %collective-permute-start = (f32[2,5,5,384]{3,2,1,0:T(8,128)}, f32[2,5,5,384]{3,2,1,0:T(8,128)S(1)}, u32[]{:S(2)}, u32[]{:S(2)}) collective-permute-start(f32[2,5,5,384]{3,2,1,0:T(8,128)} %shard_map.37), channel_id=1, source_target_pairs={{0,1},{1,2},{2,3},{3,4},{4,5},{5,6},{6,7},{7,8},{8,9},{9,10},{10,1... | collective-permute-start | bytes 230408 | tf_op jit(solution)/shard_map/ppermute | solution.py:88
  28.5 10.1 %collective-permute-start.1 = (f32[2,5,5,384]{3,2,1,0:T(8,128)S(1)}, f32[2,5,5,384]{3,2,1,0:T(8,128)S(1)}, u32[]{:S(2)}, u32[]{:S(2)}) collective-permute-start(f32[2,5,5,384]{3,2,1,0:T(8,128)S(1)} %collective-permute-done), channel_id=1, source_target_pairs={{0,1},{1,2},{2,3},{3,4},{4,5},{5,6},{6,7},{7,8},{8,9},{9,10},{10,1... | collective-permute-start | bytes 230408 | tf_op jit(solution)/shard_map/ppermute | solution.py:88
  38.7 8.4 %collective-permute-start.2 = (f32[2,5,5,384]{3,2,1,0:T(8,128)S(1)}, f32[2,5,5,384]{3,2,1,0:T(8,128)S(1)}, u32[]{:S(2)}, u32[]{:S(2)}) collective-permute-start(f32[2,5,5,384]{3,2,1,0:T(8,128)S(1)} %maximum_maximum_fusion), channel_id=1, source_target_pairs={{0,2},{1,3},{2,4},{3,5},{4,6},{5,7},{6,8},{7,9},{8,10},{9,11},{10,... | collective-permute-start | bytes 230408 | tf_op jit(solution)/shard_map/ppermute | solution.py:88
  47.2 8.8 %collective-permute-start.3 = (f32[2,5,5,384]{3,2,1,0:T(8,128)S(1)}, f32[2,5,5,384]{3,2,1,0:T(8,128)S(1)}, u32[]{:S(2)}, u32[]{:S(2)}) collective-permute-start(f32[2,5,5,384]{3,2,1,0:T(8,128)S(1)} %maximum_maximum_fusion.1), channel_id=1, source_target_pairs={{0,4},{1,5},{2,6},{3,7},{4,8},{5,9},{6,10},{7,11},{8,12},{9,13},{1... | collective-permute-start | bytes 230408 | tf_op jit(solution)/shard_map/ppermute | solution.py:88
  56.1 5.6 %collective-permute-start.4 = (f32[2,5,5,384]{3,2,1,0:T(8,128)S(1)}, f32[2,5,5,384]{3,2,1,0:T(8,128)S(1)}, u32[]{:S(2)}, u32[]{:S(2)}) collective-permute-start(f32[2,5,5,384]{3,2,1,0:T(8,128)S(1)} %maximum_maximum_fusion.2), channel_id=1, source_target_pairs={{0,8},{1,9},{2,10},{3,11},{4,12},{5,13},{6,14},{7,15},{8,16},{9,17... | collective-permute-start | bytes 230408 | tf_op jit(solution)/shard_map/ppermute | solution.py:88
  61.9 6.5 %collective-permute-start.5 = (f32[2,5,5,384]{3,2,1,0:T(8,128)S(1)}, f32[2,5,5,384]{3,2,1,0:T(8,128)S(1)}, u32[]{:S(2)}, u32[]{:S(2)}) collective-permute-start(f32[2,5,5,384]{3,2,1,0:T(8,128)S(1)} %maximum_maximum_fusion.3), channel_id=1, source_target_pairs={{0,16},{1,17},{2,18},{3,19},{4,20},{5,21},{6,22},{7,23},{8,24},{9,... | collective-permute-start | bytes 230408 | tf_op jit(solution)/shard_map/ppermute | solution.py:88
  68.5 13.2 %collective-permute-start.6 = (f32[2,5,5,384]{3,2,1,0:T(8,128)S(1)}, f32[2,5,5,384]{3,2,1,0:T(8,128)S(1)}, u32[]{:S(2)}, u32[]{:S(2)}) collective-permute-start(f32[2,5,5,384]{3,2,1,0:T(8,128)S(1)} %maximum_maximum_fusion.4), channel_id=1, source_target_pairs={{0,32},{1,33},{2,34},{3,35},{4,36},{5,37},{6,38},{7,39},{8,40},{9,... | collective-permute-start | bytes 230408 | tf_op jit(solution)/shard_map/ppermute | solution.py:88
  81.9 3.6 %collective-permute-start.7 = (f32[2,5,5,384]{3,2,1,0:T(8,128)S(1)}, f32[2,5,5,384]{3,2,1,0:T(8,128)S(1)}, u32[]{:S(2)}, u32[]{:S(2)}) collective-permute-start(f32[2,5,5,384]{3,2,1,0:T(8,128)S(1)} %maximum_maximum_fusion.5), channel_id=1, source_target_pairs={{0,64},{1,65},{2,66},{3,67},{4,68},{5,69},{6,70},{7,71},{8,72},{9,... | collective-permute-start | bytes 230408 | tf_op jit(solution)/shard_map/ppermute | solution.py:88
  85.7 4.7 %collective-permute-start.8 = (f32[2,5,5,384]{3,2,1,0:T(8,128)S(1)}, f32[2,5,5,384]{3,2,1,0:T(8,128)S(1)}, u32[]{:S(2)}, u32[]{:S(2)}) collective-permute-start(f32[2,5,5,384]{3,2,1,0:T(8,128)S(1)} %maximum_maximum_fusion.6), channel_id=1, source_target_pairs={{0,128},{1,129},{2,130},{3,131},{4,132},{5,133},{6,134},{7,135},{8... | collective-permute-start | bytes 230408 | tf_op jit(solution)/shard_map/ppermute | solution.py:88

commit v2 on v1

--- a/solution.py
+++ b/solution.py
@@ -73,19 +73,94 @@
     )
 
 
-def compose(earlier, later):
-    ex = earlier.shape[1] - 1
-    ar, ai = later[0, ex:], later[1, ex:]
-    br, bi = earlier[0], earlier[1]
-    nr = ar * br - ai * bi
-    ni = ar * bi + ai * br
-    offset = jnp.stack([nr[:ex], ni[:ex]]) + later[:, :ex]
-    gain = jnp.stack([nr[ex:], ni[ex:]])
-    return jnp.concatenate([offset, gain], axis=1)
-
-
-def shift(value, distance, count):
-    return lax.ppermute(value, AXES, [(i, (i + distance) % count) for i in range(count)])
+MESH = pl.DeviceIdType.MESH
+
+
+def shifts_of(count):
+    out, reach = [1], 1
+    while reach < count:
+        out.append(reach)
+        reach *= 2
+    return out
+
+
+def exchange_kernel(count, subs, own_ref, out_ref, recv, cur, send_sem, recv_sem):
+    ex = own_ref.shape[1] - 1
+    me = lax.axis_index("loop") * subs + lax.axis_index("sub")
+    shifts = shifts_of(count)
+
+    def device(offset):
+        t = lax.rem(me + offset + count, count)
+        return (t // subs, lax.rem(t, subs))
+
+    partners = sorted({s % count for s in shifts} | {(-s) % count for s in shifts})
+    barrier = pltpu.get_barrier_semaphore()
+    for p in partners:
+        pl.semaphore_signal(barrier, inc=1, device_id=device(p), device_id_type=MESH)
+    pl.semaphore_wait(barrier, len(partners))
+
+    for k, s in enumerate(shifts):
+        if k == 0:
+            src = own_ref
+        elif k == 1:
+            src = recv.at[0]
+        else:
+            src = cur.at[k]
+        copy = pltpu.make_async_remote_copy(
+            src_ref=src,
+            dst_ref=recv.at[k],
+            send_sem=send_sem.at[k],
+            recv_sem=recv_sem.at[k],
+            device_id=device(s),
+            device_id_type=MESH,
+        )
+        copy.start()
+        copy.wait()
+        if k == 0:
+            continue
+        later = recv.at[0] if k == 1 else cur.at[k]
+        earlier = recv.at[k]
+        ar, ai = later[0, ex], later[1, ex]
+        dst = cur.at[k + 1] if k + 1 < len(shifts) else None
+        rows = []
+        for j in range(ex + 1):
+            br, bi = earlier[0, j], earlier[1, j]
+            nr = ar * br - ai * bi
+            ni = ar * bi + ai * br
+            if j < ex:
+                nr = nr + later[0, j]
+                ni = ni + later[1, j]
+            rows.append((nr, ni))
+        if dst is not None:
+            for j, (nr, ni) in enumerate(rows):
+                dst[0, j] = nr
+                dst[1, j] = ni
+    gr, gi = rows[ex]
+    denom_re = 1.0 - gr
+    denom_im = -gi
+    size = denom_re * denom_re + denom_im * denom_im
+    for j in range(ex):
+        br, bi = rows[j]
+        out_ref[0, j] = (br * denom_re + bi * denom_im) / size
+        out_ref[1, j] = (bi * denom_re - br * denom_im) / size
+
+
+def entering_state(own, count, subs):
+    two, slots, fields, wall = own.shape
+    rounds = len(shifts_of(count))
+    return pl.pallas_call(
+        functools.partial(exchange_kernel, count, subs),
+        out_shape=jax.ShapeDtypeStruct((two, slots - 1, fields, wall), jnp.float32),
+        in_specs=[pl.BlockSpec(memory_space=pltpu.VMEM)],
+        out_specs=pl.BlockSpec(memory_space=pltpu.VMEM),
+        scratch_shapes=[
+            pltpu.VMEM((rounds,) + own.shape, jnp.float32),
+            pltpu.VMEM((rounds,) + own.shape, jnp.float32),
+            pltpu.SemaphoreType.DMA((rounds,)),
+            pltpu.SemaphoreType.DMA((rounds,)),
+        ],
+        compiler_params=pltpu.CompilerParams(collective_id=0, has_side_effects=True),
+    )(own)
 
 
 def local(rate, phase, forcing):
@@ -108,20 +183,7 @@
         map_kernel, jax.ShapeDtypeStruct((2, ex + 1, fields, wall), jnp.float32), 3
     )(coef, scale, forcing)
 
-    loop_map = shift(own, 1, count)
-    reach = 1
-    while reach < count:
-        loop_map = compose(shift(loop_map, reach, count), loop_map)
-        reach *= 2
-
-    gr, gi = loop_map[0, ex], loop_map[1, ex]
-    denom_re = 1.0 - gr
-    denom_im = -gi
-    size = denom_re * denom_re + denom_im * denom_im
-    br, bi = loop_map[0, :ex], loop_map[1, :ex]
-    entering = jnp.stack(
-        [(br * denom_re + bi * denom_im) / size, (bi * denom_re - br * denom_im) / size]
-    )
+    entering = entering_state(own, count, lax.axis_size("sub"))
 
     return vmem_call(
         march_kernel, jax.ShapeDtypeStruct(forcing.shape, jnp.float32), 4

time: 100 us -> 79.1 us (0.79)
  waiting for transfers between devices: 68.4 us -> 0 us
  Pallas kernels: 7.99 us -> 65.7 us
  starting transfers between devices: 7.64 us -> 0 us
  local copies, waits for them, and re-layouts: 8 us -> 6.32 us
    ppermute x9 -> x0, waiting for transfers between devices: 68.4 us -> none  [shift(): lax.ppermute(value, AXES, [(i, (i + distance) % count) for i in range(cou...]
    pallas_call x0 -> x1, Pallas kernels: none -> 57.7 us  [entering_state(): pl.pallas_call(functools.partial(exchange_kernel, count, subs), out_shape...]
    ppermute x9 -> x0, starting transfers between devices: 7.64 us -> none  [shift(): lax.ppermute(value, AXES, [(i, (i + distance) % count) for i in range(cou...]
    unnamed x3, local copies, waits for them, and re-layouts: 4.34 us -> 2.81 us
    another operation x2, other arithmetic: 2.49 us -> 3.55 us  [local(): coef = jnp.stack([magnitude * jnp.cos(phase), magnitude * jnp.sin(phase)])]
  transfers between devices with their start and end apart: 9 -> 0, of which waited for: 9 -> 0; matrix products, arithmetic and copies ran while one was open for 0% -> 0% of each run, Pallas kernels for 0% -> 0%
where the time goes in v2:
time: 79.1 us; the launch traced here: 78.7 us
  Pallas kernels  65.7 us (83%)
  other arithmetic  6.64 us (8%)
  local copies, waits for them, and re-layouts  6.32 us (8%)
    pallas_call x1, Pallas kernels, entering_state(): pl.pallas_call(functools.partial(exchange_kernel, count, subs), out_shape...  57.7 us
    pallas_call x1, Pallas kernels, local(): vmem_call(march_kernel, jax.ShapeDtypeStruct(forcing.shape, jnp.float32), 4)  4.48 us
    another operation x2, other arithmetic, local(): coef = jnp.stack([magnitude * jnp.cos(phase), magnitude * jnp.sin(phase)])  3.55 us
    pallas_call x1, Pallas kernels, local(): vmem_call(map_kernel, jax.ShapeDtypeStruct((2, ex + 1, fields, wall), jnp...  3.52 us
    pallas_call x1, local copies, waits for them, and re-layouts, local(): vmem_call(march_kernel, jax.ShapeDtypeStruct(forcing.shape, jnp.float32), 4)  3.51 us
    unnamed x3, local copies, waits for them, and re-layouts  2.81 us
    sqrt x1, other arithmetic, local(): scale = jnp.sqrt(-jnp.expm1(-2.0 * rate))  1.99 us

profile of v2, /device:TPU:1, one launch (start us, length us, event | category | flops | bytes accessed | tf_op | source)
XLA Modules:
  0.0 78.7 jit_solution(6959054980846639257)
XLA Ops:
  0.0 0.0 copy-start
  0.0 1.1 %neg.6 = f32[32,5,384]{2,0,1:T(8,128)S(1)} negate(f32[32,5,384]{2,0,1:T(8,128)} %param.3) | non-fusion elementwise | flops 61440 | bytes 491520 | tf_op jit(solution)/shard_map/neg | solution.py:178
  1.1 2.0 %fusion.6.scale_ref = f32[32,5,384]{2,1,0:T(8,128)} fusion(f32[32,5,384]{2,0,1:T(8,128)} %param.3), kind=kLoop, calls=%fused_computation.10 | loop fusion | flops 122880 | bytes 491520 | tf_op jit(solution)/shard_map/sqrt | solution.py:180
  3.1 2.6 %fusion.1 = (f32[1,32,5,384]{3,2,1,0:T(8,128)S(1)}, f32[1,32,5,384]{3,2,1,0:T(8,128)S(1)}) fusion(f32[32,5,384]{2,0,1:T(8,128)} %param.4, f32[32,5,384]{2,0,1:T(8,128)S(1)} %neg.6, f32[32]{0:T(128)S(1)} %compare_select_fusion), kind=kLoop, calls=%fused_computation.4 | loop fusion | flops 184320 | bytes 983168 | tf_op jit(solution)/shard_map/stack | solution.py:179
  5.7 1.0 %pad_maximum_fusion.coef_ref = f32[2,32,5,384]{3,2,1,0:T(8,128)} fusion(f32[1,32,5,384]{3,2,1,0:T(8,128)S(1)} %get-tuple-element.6, f32[1,32,5,384]{3,2,1,0:T(8,128)S(1)} %get-tuple-element.5), kind=kLoop, calls=%fused_computation | loop fusion | flops 122880 | bytes 983040 | tf_op jit(solution)/shard_map/stack | solution.py:179
  6.7 0.0 copy-done
  6.7 2.8 %copy.16.f_ref = f32[2,4,32,5,384]{4,3,2,1,0:T(8,128)} copy(f32[2,4,32,5,384]{4,2,3,1,0:T(8,128)S(1)} %copy-done) | data formatting | bytes 3932160 | tf_op args[2]
  9.5 3.5 %shard_map.37.own_ref = f32[2,5,5,384]{3,2,1,0:T(8,128)} custom-call(f32[2,32,5,384]{3,2,1,0:T(8,128)} %pad_maximum_fusion.coef_ref, f32[32,5,384]{2,1,0:T(8,128)} %fusion.6.scale_ref, f32[2,4,32,5,384]{4,3,2,1,0:T(8,128)} %copy.16.f_ref), custom_call_target="tpu_custom_call" | custom-call | tf_op jit(solution)/shard_map/pallas_call | solution.py:182
  13.0 57.7 %shard_map.38.x0_ref = f32[2,4,5,384]{3,2,1,0:T(8,128)} custom-call(f32[2,5,5,384]{3,2,1,0:T(8,128)} %shard_map.37.own_ref), custom_call_target="tpu_custom_call" | custom-call | tf_op jit(solution)/shard_map/pallas_call | solution.py:151
  70.7 4.5 %shard_map.39 = f32[2,4,32,5,384]{4,3,2,1,0:T(8,128)} custom-call(f32[2,32,5,384]{3,2,1,0:T(8,128)} %pad_maximum_fusion.coef_ref, f32[32,5,384]{2,1,0:T(8,128)} %fusion.6.scale_ref, f32[2,4,32,5,384]{4,3,2,1,0:T(8,128)} %copy.16.f_ref, f32[2,4,5,384]{3,2,1,0:T(8,128)} %shard_map.38.x0_ref), custom_call_target="tpu_custom_call" | custom-call | tf_op jit(solution)/shard_map/pallas_call | solution.py:188
  75.2 3.5 %copy.17 = f32[2,4,32,5,384]{4,2,3,1,0:T(8,128)} copy(f32[2,4,32,5,384]{4,3,2,1,0:T(8,128)} %shard_map.39) | data formatting | bytes 3932160 | tf_op jit(solution)/shard_map/pallas_call | solution.py:188
  (1 shorter events, 0.0 us)
Async XLA Ops:
  0.0 6.7 %copy-start = (f32[2,4,32,5,384]{4,2,3,1,0:T(8,128)S(1)}, f32[2,4,32,5,384]{4,2,3,1,0:T(8,128)}, u32[]{:S(2)}) copy-start(f32[2,4,32,5,384]{4,2,3,1,0:T(8,128)} %param.5) | copy-start | bytes 5898244

commit v3 on v2

--- a/solution.py
+++ b/solution.py
@@ -76,88 +76,105 @@
 MESH = pl.DeviceIdType.MESH
 
 
-def shifts_of(count):
-    out, reach = [1], 1
+def rounds_of(count):
+    out, reach = [], 1
     while reach < count:
-        out.append(reach)
-        reach *= 2
+        fan = 4 if count % (reach * 4) == 0 else 2
+        out.append((reach, fan))
+        reach *= fan
     return out
+
+
+def slots_of(count):
+    slots = []
+    for k, (stride, fan) in enumerate(rounds_of(count)):
+        for j in range(1, fan + (1 if k == 0 else 0)):
+            slots.append((k, j * stride))
+    return slots
 
 
 def exchange_kernel(count, subs, own_ref, out_ref, recv, cur, send_sem, recv_sem):
     ex = own_ref.shape[1] - 1
     me = lax.axis_index("loop") * subs + lax.axis_index("sub")
-    shifts = shifts_of(count)
+    rounds = rounds_of(count)
+    slots = slots_of(count)
 
     def device(offset):
         t = lax.rem(me + offset + count, count)
         return (t // subs, lax.rem(t, subs))
 
-    partners = sorted({s % count for s in shifts} | {(-s) % count for s in shifts})
+    partners = sorted({o % count for _, o in slots} | {(-o) % count for _, o in slots})
     barrier = pltpu.get_barrier_semaphore()
     for p in partners:
         pl.semaphore_signal(barrier, inc=1, device_id=device(p), device_id_type=MESH)
     pl.semaphore_wait(barrier, len(partners))
 
-    for k, s in enumerate(shifts):
-        if k == 0:
-            src = own_ref
-        elif k == 1:
-            src = recv.at[0]
-        else:
-            src = cur.at[k]
-        copy = pltpu.make_async_remote_copy(
-            src_ref=src,
-            dst_ref=recv.at[k],
-            send_sem=send_sem.at[k],
-            recv_sem=recv_sem.at[k],
-            device_id=device(s),
-            device_id_type=MESH,
-        )
-        copy.start()
-        copy.wait()
-        if k == 0:
-            continue
-        later = recv.at[0] if k == 1 else cur.at[k]
-        earlier = recv.at[k]
-        ar, ai = later[0, ex], later[1, ex]
-        dst = cur.at[k + 1] if k + 1 < len(shifts) else None
+    def load(ref):
+        return [(ref[0, j], ref[1, j]) for j in range(ex + 1)]
+
+    def compose(earlier, later):
+        ar, ai = later[ex]
         rows = []
         for j in range(ex + 1):
-            br, bi = earlier[0, j], earlier[1, j]
+            br, bi = earlier[j]
             nr = ar * br - ai * bi
             ni = ar * bi + ai * br
             if j < ex:
-                nr = nr + later[0, j]
-                ni = ni + later[1, j]
+                nr = nr + later[j][0]
+                ni = ni + later[j][1]
             rows.append((nr, ni))
-        if dst is not None:
-            for j, (nr, ni) in enumerate(rows):
+        return rows
+
+    held = None
+    for k, (stride, fan) in enumerate(rounds):
+        mine = [i for i, (r, _) in enumerate(slots) if r == k]
+        src = own_ref if k == 0 else cur.at[k]
+        copies = []
+        for i in mine:
+            copy = pltpu.make_async_remote_copy(
+                src_ref=src,
+                dst_ref=recv.at[i],
+                send_sem=send_sem.at[i],
+                recv_sem=recv_sem.at[i],
+                device_id=device(slots[i][1]),
+                device_id_type=MESH,
+            )
+            copy.start()
+            copies.append(copy)
+        for n, (i, copy) in enumerate(zip(mine, copies)):
+            copy.wait()
+            arrived = load(recv.at[i])
+            held = arrived if (k == 0 and n == 0) else compose(arrived, held)
+        if k + 1 < len(rounds):
+            dst = cur.at[k + 1]
+            for j, (nr, ni) in enumerate(held):
                 dst[0, j] = nr
                 dst[1, j] = ni
-    gr, gi = rows[ex]
+            held = load(dst)
+    gr, gi = held[ex]
     denom_re = 1.0 - gr
     denom_im = -gi
     size = denom_re * denom_re + denom_im * denom_im
     for j in range(ex):
-        br, bi = rows[j]
+        br, bi = held[j]
         out_ref[0, j] = (br * denom_re + bi * denom_im) / size
         out_ref[1, j] = (bi * denom_re - br * denom_im) / size
 
 
 def entering_state(own, count, subs):
     two, slots, fields, wall = own.shape
-    rounds = len(shifts_of(count))
+    n_slots = len(slots_of(count))
+    n_rounds = len(rounds_of(count))
     return pl.pallas_call(
         functools.partial(exchange_kernel, count, subs),
         out_shape=jax.ShapeDtypeStruct((two, slots - 1, fields, wall), jnp.float32),
         in_specs=[pl.BlockSpec(memory_space=pltpu.VMEM)],
         out_specs=pl.BlockSpec(memory_space=pltpu.VMEM),
         scratch_shapes=[
-            pltpu.VMEM((rounds,) + own.shape, jnp.float32),
-            pltpu.VMEM((rounds,) + own.shape, jnp.float32),
-            pltpu.SemaphoreType.DMA((rounds,)),
-            pltpu.SemaphoreType.DMA((rounds,)),
+            pltpu.VMEM((n_slots,) + own.shape, jnp.float32),
+            pltpu.VMEM((n_rounds,) + own.shape, jnp.float32),
+            pltpu.SemaphoreType.DMA((n_slots,)),
+            pltpu.SemaphoreType.DMA((n_slots,)),
         ],
         compiler_params=pltpu.CompilerParams(collective_id=0, has_side_effects=True),
     )(own)

time: 79.1 us -> 76.9 us (0.972)
  Pallas kernels: 65.7 us -> 63.7 us
    pallas_call x1, Pallas kernels: 57.7 us -> 55.7 us  [entering_state(): pl.pallas_call(functools.partial(exchange_kernel, count, subs), out_shape...]
where the time goes in v3:
time: 76.9 us; the launch traced here: 76.7 us
  Pallas kernels  63.7 us (83%)
  other arithmetic  6.64 us (9%)
  local copies, waits for them, and re-layouts  6.32 us (8%)
    pallas_call x1, Pallas kernels, entering_state(): pl.pallas_call(functools.partial(exchange_kernel, count, subs), out_shape...  55.7 us
    pallas_call x1, Pallas kernels, local(): vmem_call(march_kernel, jax.ShapeDtypeStruct(forcing.shape, jnp.float32), 4)  4.48 us
    another operation x2, other arithmetic, local(): coef = jnp.stack([magnitude * jnp.cos(phase), magnitude * jnp.sin(phase)])  3.55 us
    pallas_call x1, Pallas kernels, local(): vmem_call(map_kernel, jax.ShapeDtypeStruct((2, ex + 1, fields, wall), jnp...  3.52 us
    pallas_call x1, local copies, waits for them, and re-layouts, local(): vmem_call(march_kernel, jax.ShapeDtypeStruct(forcing.shape, jnp.float32), 4)  3.51 us
    unnamed x3, local copies, waits for them, and re-layouts  2.81 us
    sqrt x1, other arithmetic, local(): scale = jnp.sqrt(-jnp.expm1(-2.0 * rate))  1.99 us

profile of v3, /device:TPU:1, one launch (start us, length us, event | category | flops | bytes accessed | tf_op | source)
XLA Modules:
  0.0 76.7 jit_solution(17278611819655777354)
XLA Ops:
  0.0 0.0 copy-start
  0.0 1.1 %neg.6 = f32[32,5,384]{2,0,1:T(8,128)S(1)} negate(f32[32,5,384]{2,0,1:T(8,128)} %param.3) | non-fusion elementwise | flops 61440 | bytes 491520 | tf_op jit(solution)/shard_map/neg | solution.py:195
  1.1 2.0 %fusion.6.scale_ref = f32[32,5,384]{2,1,0:T(8,128)} fusion(f32[32,5,384]{2,0,1:T(8,128)} %param.3), kind=kLoop, calls=%fused_computation.10 | loop fusion | flops 122880 | bytes 491520 | tf_op jit(solution)/shard_map/sqrt | solution.py:197
  3.1 2.6 %fusion.1 = (f32[1,32,5,384]{3,2,1,0:T(8,128)S(1)}, f32[1,32,5,384]{3,2,1,0:T(8,128)S(1)}) fusion(f32[32,5,384]{2,0,1:T(8,128)} %param.4, f32[32,5,384]{2,0,1:T(8,128)S(1)} %neg.6, f32[32]{0:T(128)S(1)} %compare_select_fusion), kind=kLoop, calls=%fused_computation.4 | loop fusion | flops 184320 | bytes 983168 | tf_op jit(solution)/shard_map/stack | solution.py:196
  5.7 1.0 %pad_maximum_fusion.coef_ref = f32[2,32,5,384]{3,2,1,0:T(8,128)} fusion(f32[1,32,5,384]{3,2,1,0:T(8,128)S(1)} %get-tuple-element.6, f32[1,32,5,384]{3,2,1,0:T(8,128)S(1)} %get-tuple-element.5), kind=kLoop, calls=%fused_computation | loop fusion | flops 122880 | bytes 983040 | tf_op jit(solution)/shard_map/stack | solution.py:196
  6.7 0.0 copy-done
  6.7 2.8 %copy.16.f_ref = f32[2,4,32,5,384]{4,3,2,1,0:T(8,128)} copy(f32[2,4,32,5,384]{4,2,3,1,0:T(8,128)S(1)} %copy-done) | data formatting | bytes 3932160 | tf_op args[2]
  9.5 3.5 %shard_map.37.own_ref = f32[2,5,5,384]{3,2,1,0:T(8,128)} custom-call(f32[2,32,5,384]{3,2,1,0:T(8,128)} %pad_maximum_fusion.coef_ref, f32[32,5,384]{2,1,0:T(8,128)} %fusion.6.scale_ref, f32[2,4,32,5,384]{4,3,2,1,0:T(8,128)} %copy.16.f_ref), custom_call_target="tpu_custom_call" | custom-call | tf_op jit(solution)/shard_map/pallas_call | solution.py:199
  13.0 55.7 %shard_map.38.x0_ref = f32[2,4,5,384]{3,2,1,0:T(8,128)} custom-call(f32[2,5,5,384]{3,2,1,0:T(8,128)} %shard_map.37.own_ref), custom_call_target="tpu_custom_call" | custom-call | tf_op jit(solution)/shard_map/pallas_call | solution.py:168
  68.7 4.5 %shard_map.39 = f32[2,4,32,5,384]{4,3,2,1,0:T(8,128)} custom-call(f32[2,32,5,384]{3,2,1,0:T(8,128)} %pad_maximum_fusion.coef_ref, f32[32,5,384]{2,1,0:T(8,128)} %fusion.6.scale_ref, f32[2,4,32,5,384]{4,3,2,1,0:T(8,128)} %copy.16.f_ref, f32[2,4,5,384]{3,2,1,0:T(8,128)} %shard_map.38.x0_ref), custom_call_target="tpu_custom_call" | custom-call | tf_op jit(solution)/shard_map/pallas_call | solution.py:205
  73.1 3.5 %copy.17 = f32[2,4,32,5,384]{4,2,3,1,0:T(8,128)} copy(f32[2,4,32,5,384]{4,3,2,1,0:T(8,128)} %shard_map.39) | data formatting | bytes 3932160 | tf_op jit(solution)/shard_map/pallas_call | solution.py:205
  (1 shorter events, 0.0 us)
Async XLA Ops:
  0.0 6.7 %copy-start = (f32[2,4,32,5,384]{4,2,3,1,0:T(8,128)S(1)}, f32[2,4,32,5,384]{4,2,3,1,0:T(8,128)}, u32[]{:S(2)}) copy-start(f32[2,4,32,5,384]{4,2,3,1,0:T(8,128)} %param.5) | copy-start | bytes 5898244

commit v4 on v3

v4 whole, which is shorter than its diff:
```python
import functools

import jax
import jax.numpy as jnp
from jax import lax
from jax.experimental import pallas as pl
from jax.experimental.pallas import tpu as pltpu
from jax.sharding import PartitionSpec as P

fringe_total = 0.7
FRINGE_STATIONS = 32
AXES = ("loop", "sub")
MESH = pl.DeviceIdType.MESH
LANES = 128


def rounds_of(count):
    out, reach = [], 1
    while reach < count:
        fan = 4 if count % (reach * 4) == 0 else 2
        out.append((reach, fan))
        reach *= fan
    return out


def slots_of(count):
    slots = []
    for k, (stride, fan) in enumerate(rounds_of(count)):
        for j in range(1, fan + (1 if k == 0 else 0)):
            slots.append((k, j * stride))
    return slots


def expm1(x):
    u = jnp.exp(x)
    return jnp.where(u == 1.0, x, (u - 1.0) * x / jnp.log(u))


def fetch(srcs, bufs, sems):
    copies = []
    for n, (src, buf) in enumerate(zip(srcs, bufs)):
        for q in range(buf.shape[0]):
            copy = pltpu.make_async_copy(
                src.at[:, pl.ds(q * LANES, LANES)], buf.at[q], sems.at[n * buf.shape[0] + q]
            )
            copy.start()
            copies.append(copy)
    return copies


def station(buf, i, fields, stations):
    rows = pl.ds(i, fields, stride=stations)
    return jnp.concatenate([buf[q, rows, :] for q in range(buf.shape[0])], axis=1)


def map_kernel(count, subs, rate_hbm, phase_hbm, f_hbm, coef_ref, x0_ref,
               rbuf, pbuf, fbuf, in_sem, tmp, pack, recv, cur, send_sem, recv_sem):
    ex = x0_ref.shape[1]
    stations, fields, wall = coef_ref.shape[1:]
    chunks = wall // LANES
    copies = fetch(
        [rate_hbm, phase_hbm] + [f_hbm.at[n] for n in range(2 * ex)],
        [rbuf, pbuf] + [fbuf.at[n] for n in range(2 * ex)],
        in_sem,
    )
    me = lax.axis_index("loop") * subs + lax.axis_index("sub")
    rounds = rounds_of(count)
    slots = slots_of(count)

    def device(offset):
        t = lax.rem(me + offset + count, count)
        return (t // subs, lax.rem(t, subs))

    partners = sorted({o % count for _, o in slots} | {(-o) % count for _, o in slots})
    barrier = pltpu.get_barrier_semaphore()
    for p in partners:
        pl.semaphore_signal(barrier, inc=1, device_id=device(p), device_id_type=MESH)

    first_fringe = count * stations - FRINGE_STATIONS
    damp = jnp.float32(fringe_total ** (1.0 / FRINGE_STATIONS))
    for copy in copies:
        copy.wait()

    def step(i, carry):
        pr, pi, xr, xi = carry
        r = station(rbuf, i, fields, stations)
        ph = station(pbuf, i, fields, stations)
        sponge = jnp.where(me * stations + i >= first_fringe, damp, jnp.float32(1.0))
        mag = jnp.exp(-r) * sponge
        cr = mag * jnp.cos(ph)
        ci = mag * jnp.sin(ph)
        sc = jnp.sqrt(-expm1(-2.0 * r))
        coef_ref[0, i] = cr
        coef_ref[1, i] = ci
        coef_ref[2, i] = sc
        npr = cr * pr - ci * pi
        npi = cr * pi + ci * pr
        nxr, nxi = [], []
        for e in range(ex):
            fr = station(fbuf.at[e], i, fields, stations)
            fi = station(fbuf.at[ex + e], i, fields, stations)
            nxr.append(cr * xr[e] - ci * xi[e] + sc * fr)
            nxi.append(cr * xi[e] + ci * xr[e] + sc * fi)
        return npr, npi, tuple(nxr), tuple(nxi)

    shape = (fields, wall)
    one = jnp.ones(shape, jnp.float32)
    zero = jnp.zeros(shape, jnp.float32)
    init = (one, zero, (zero,) * ex, (zero,) * ex)
    pr, pi, xr, xi = lax.fori_loop(0, stations, step, init, unroll=4)

    values = [(xr[e], xi[e]) for e in range(ex)] + [(pr, pi)]
    for j, pair in enumerate(values):
        for c in range(2):
            tmp[...] = pair[c]
            for f in range(fields):
                for q in range(chunks):
                    pack[c, j, pl.ds(f * chunks + q, 1), :] = tmp[
                        pl.ds(f, 1), pl.ds(q * LANES, LANES)
                    ]

    pl.semaphore_wait(barrier, len(partners))

    def load(ref):
        return [(ref[0, j], ref[1, j]) for j in range(ex + 1)]

    def compose(earlier, later):
        ar, ai = later[ex]
        out = []
        for j in range(ex + 1):
            br, bi = earlier[j]
            nr = ar * br - ai * bi
            ni = ar * bi + ai * br
            if j < ex:
                nr = nr + later[j][0]
                ni = ni + later[j][1]
            out.append((nr, ni))
        return out

    held = None
    for k in range(len(rounds)):
        mine = [i for i, (r, _) in enumerate(slots) if r == k]
        src = pack if k == 0 else cur.at[k]
        copies = []
        for i in mine:
            copy = pltpu.make_async_remote_copy(
                src_ref=src,
                dst_ref=recv.at[i],
                send_sem=send_sem.at[i],
                recv_sem=recv_sem.at[i],
                device_id=device(slots[i][1]),
                device_id_type=MESH,
            )
            copy.start()
            copies.append(copy)
        for n, (i, copy) in enumerate(zip(mine, copies)):
            copy.wait()
            arrived = load(recv.at[i])
            held = arrived if (k == 0 and n == 0) else compose(arrived, held)
        if k + 1 < len(rounds):
            dst = cur.at[k + 1]
            for j, (nr, ni) in enumerate(held):
                dst[0, j] = nr
                dst[1, j] = ni
            held = load(dst)

    gr, gi = held[ex]
    denom_re = 1.0 - gr
    denom_im = -gi
    size = denom_re * denom_re + denom_im * denom_im
    ent = cur.at[0]
    for j in range(ex):
        br, bi = held[j]
        ent[0, j] = (br * denom_re + bi * denom_im) / size
        ent[1, j] = (bi * denom_re - br * denom_im) / size
    for c in range(2):
        for e in range(ex):
            for f in range(fields):
                for q in range(chunks):
                    x0_ref[c, e, pl.ds(f, 1), pl.ds(q * LANES, LANES)] = ent[
                        c, e, pl.ds(f * chunks + q, 1), :
                    ]


def march_kernel(coef_ref, f_hbm, x0_ref, out_hbm, fbuf, obuf, in_sem, out_sem):
    ex = x0_ref.shape[1]
    stations, fields = coef_ref.shape[1:3]
    chunks = fbuf.shape[1]
    copies = fetch([f_hbm.at[n] for n in range(2 * ex)], [fbuf.at[n] for n in range(2 * ex)], in_sem)
    for copy in copies:
        copy.wait()

    def put(n, i, value):
        rows = pl.ds(i, fields, stride=stations)
        for q in range(chunks):
            obuf[n, q, rows, :] = value[:, q * LANES:(q + 1) * LANES]

    def step(i, carry):
        xr, xi = carry
        cr = coef_ref[0, i]
        ci = coef_ref[1, i]
        sc = coef_ref[2, i]
        nxr, nxi = [], []
        for e in range(ex):
            fr = station(fbuf.at[e], i, fields, stations)
            fi = station(fbuf.at[ex + e], i, fields, stations)
            r = cr * xr[e] - ci * xi[e] + sc * fr
            m = cr * xi[e] + ci * xr[e] + sc * fi
            put(e, i, r)
            put(ex + e, i, m)
            nxr.append(r)
            nxi.append(m)
        return tuple(nxr), tuple(nxi)

    init = (tuple(x0_ref[0, e] for e in range(ex)), tuple(x0_ref[1, e] for e in range(ex)))
    lax.fori_loop(0, stations, step, init, unroll=4)
    copies = []
    for n in range(2 * ex):
        for q in range(chunks):
            copy = pltpu.make_async_copy(
                obuf.at[n, q], out_hbm.at[n, :, pl.ds(q * LANES, LANES)], out_sem.at[n * chunks + q]
            )
            copy.start()
            copies.append(copy)
    for copy in copies:
        copy.wait()


def local(rate, phase, forcing):
    stations, fields, wall = rate.shape
    two, ex = forcing.shape[:2]
    count = lax.axis_size(AXES)
    subs = lax.axis_size("sub")
    rate_t = jnp.transpose(rate, (1, 0, 2)).reshape(fields * stations, wall)
    phase_t = jnp.transpose(phase, (1, 0, 2)).reshape(fields * stations, wall)
    forcing_t = jnp.transpose(forcing, (0, 1, 3, 2, 4)).reshape(
        two * ex, fields * stations, wall
    )
    n_slots = len(slots_of(count))
    n_rounds = len(rounds_of(count))
    packed = (2, ex + 1, fields * wall // LANES, LANES)
    vmem = pl.BlockSpec(memory_space=pltpu.VMEM)
    hbm = pl.BlockSpec(memory_space=pl.ANY)
    chunks = wall // LANES
    slab = (fields * stations, LANES)
    fbuf = pltpu.VMEM((two * ex, chunks) + slab, jnp.float32)
    coef, x0 = pl.pallas_call(
        functools.partial(map_kernel, count, subs),
        out_shape=(
            jax.ShapeDtypeStruct((3, stations, fields, wall), jnp.float32),
            jax.ShapeDtypeStruct((2, ex, fields, wall), jnp.float32),
        ),
        in_specs=[hbm] * 3,
        out_specs=(vmem, vmem),
        scratch_shapes=[
            pltpu.VMEM((chunks,) + slab, jnp.float32),
            pltpu.VMEM((chunks,) + slab, jnp.float32),
            fbuf,
            pltpu.SemaphoreType.DMA(((2 + two * ex) * chunks,)),
            pltpu.VMEM((fields, wall), jnp.float32),
            pltpu.VMEM(packed, jnp.float32),
            pltpu.VMEM((n_slots,) + packed, jnp.float32),
            pltpu.VMEM((n_rounds,) + packed, jnp.float32),
            pltpu.SemaphoreType.DMA((n_slots,)),
            pltpu.SemaphoreType.DMA((n_slots,)),
        ],
        compiler_params=pltpu.CompilerParams(collective_id=0, has_side_effects=True),
    )(rate_t, phase_t, forcing_t)
    out_t = pl.pallas_call(
        march_kernel,
        out_shape=jax.ShapeDtypeStruct(forcing_t.shape, jnp.float32),
        in_specs=[vmem, hbm, vmem],
        out_specs=hbm,
        scratch_shapes=[
            fbuf,
            fbuf,
            pltpu.SemaphoreType.DMA((two * ex * chunks,)),
            pltpu.SemaphoreType.DMA((two * ex * chunks,)),
        ],
    )(coef, forcing_t, x0)
    return jnp.transpose(out_t.reshape(two, ex, fields, stations, wall), (0, 1, 3, 2, 4))


def solution(mesh):
    count = mesh.shape["loop"] * mesh.shape["sub"]
    assert count & (count - 1) == 0
    placed = (
        P(AXES, None, None),
        P(AXES, None, None),
        P(None, None, AXES, None, None),
    )
    return jax.shard_map(
        local,
        mesh=mesh,
        in_specs=placed,
        out_specs=P(None, None, AXES, None, None),
        check_vma=False,
    )
```

time: 76.9 us -> 49.8 us (0.65)
  Pallas kernels: 63.7 us -> 49.5 us
  other arithmetic: 6.64 us -> 0 us
  local copies, waits for them, and re-layouts: 6.32 us -> 0 us
    pallas_call x3 -> x2, Pallas kernels: 63.7 us -> 49.5 us  [the longest x1 42.4 us: local(): pl.pallas_call(functools.partial(map_kernel, count, subs), out_shape=(jax...]
    another operation x2 -> x0, other arithmetic: 3.55 us -> none  [local(): coef = jnp.stack([magnitude * jnp.cos(phase), magnitude * jnp.sin(phase)])]
    pallas_call x1 -> x0, local copies, waits for them, and re-layouts: 3.51 us -> none  [local(): vmem_call(march_kernel, jax.ShapeDtypeStruct(forcing.shape, jnp.float32), 4)]
    unnamed x3 -> x0, local copies, waits for them, and re-layouts: 2.81 us -> none
    sqrt x1 -> x0, other arithmetic: 1.99 us -> none  [local(): scale = jnp.sqrt(-jnp.expm1(-2.0 * rate))]
    neg x1 -> x0, other arithmetic: 1.1 us -> none  [local(): magnitude = jnp.exp(-rate) * sponge[:, None, None]]
where the time goes in v4:
time: 49.8 us; the launch traced here: 49.6 us
  Pallas kernels  49.5 us (99%)
    pallas_call x1, Pallas kernels, local(): pl.pallas_call(functools.partial(map_kernel, count, subs), out_shape=(jax...  42.4 us
    pallas_call x1, Pallas kernels, local(): pl.pallas_call(march_kernel, out_shape=jax.ShapeDtypeStruct(forcing_t.sha...  7.15 us

profile of v4, /device:TPU:1, one launch (start us, length us, event | category | flops | bytes accessed | tf_op | source)
XLA Modules:
  0.0 49.6 jit_solution(1455063095095240909)
XLA Ops:
  0.0 42.4 %shard_map.37 = (f32[3,32,5,384]{3,2,1,0:T(8,128)}, f32[2,4,5,384]{3,2,1,0:T(8,128)}) custom-call(f32[160,384]{1,0:T(8,128)} %bitcast.14, f32[160,384]{1,0:T(8,128)} %bitcast.15, f32[8,160,384]{2,1,0:T(8,128)} %bitcast.12), custom_call_target="tpu_custom_call" | custom-call | tf_op jit(solution)/shard_map/pallas_call | solution.py:247
  42.4 7.2 %shard_map.38 = f32[8,160,384]{2,1,0:T(8,128)} custom-call(f32[3,32,5,384]{3,2,1,0:T(8,128)} %get-tuple-element.7.coef_ref, f32[8,160,384]{2,1,0:T(8,128)} %bitcast.13, f32[2,4,5,384]{3,2,1,0:T(8,128)} %get-tuple-element.8.x0_ref), custom_call_target="tpu_custom_call" | custom-call | tf_op jit(solution)/shard_map/pallas_call | solution.py:269

commit v5 on v4

--- a/solution.py
+++ b/solution.py
@@ -53,8 +53,9 @@
     return jnp.concatenate([buf[q, rows, :] for q in range(buf.shape[0])], axis=1)
 
 
-def map_kernel(count, subs, rate_hbm, phase_hbm, f_hbm, coef_ref, x0_ref,
-               rbuf, pbuf, fbuf, in_sem, tmp, pack, recv, cur, send_sem, recv_sem):
+def resolvent_kernel(count, subs, rate_hbm, phase_hbm, f_hbm, out_hbm,
+                     rbuf, pbuf, fbuf, in_sem, coef_ref, x0_ref, qbuf, gbuf, out_sem,
+                     tmp, pack, recv, cur, send_sem, recv_sem):
     ex = x0_ref.shape[1]
     stations, fields, wall = coef_ref.shape[1:]
     chunks = wall // LANES
@@ -121,6 +122,35 @@
 
     pl.semaphore_wait(barrier, len(partners))
 
+    def put(buf, n, i, value):
+        rows = pl.ds(i, fields, stride=stations)
+        for q in range(chunks):
+            buf[n, q, rows, :] = value[:, q * LANES:(q + 1) * LANES]
+
+    def local_march():
+        def step(i, carry):
+            pr, pi, xr, xi = carry
+            cr = coef_ref[0, i]
+            ci = coef_ref[1, i]
+            sc = coef_ref[2, i]
+            npr = cr * pr - ci * pi
+            npi = cr * pi + ci * pr
+            put(gbuf, 0, i, npr)
+            put(gbuf, 1, i, npi)
+            nxr, nxi = [], []
+            for e in range(ex):
+                fr = station(fbuf.at[e], i, fields, stations)
+                fi = station(fbuf.at[ex + e], i, fields, stations)
+                r = cr * xr[e] - ci * xi[e] + sc * fr
+                m = cr * xi[e] + ci * xr[e] + sc * fi
+                put(qbuf, e, i, r)
+                put(qbuf, ex + e, i, m)
+                nxr.append(r)
+                nxi.append(m)
+            return npr, npi, tuple(nxr), tuple(nxi)
+
+        lax.fori_loop(0, stations, step, init, unroll=4)
+
     def load(ref):
         return [(ref[0, j], ref[1, j]) for j in range(ex + 1)]
 
@@ -153,6 +183,8 @@
             )
             copy.start()
             copies.append(copy)
+        if k == 0:
+            local_march()
         for n, (i, copy) in enumerate(zip(mine, copies)):
             copy.wait()
             arrived = load(recv.at[i])
@@ -181,47 +213,24 @@
                         c, e, pl.ds(f * chunks + q, 1), :
                     ]
 
-
-def march_kernel(coef_ref, f_hbm, x0_ref, out_hbm, fbuf, obuf, in_sem, out_sem):
-    ex = x0_ref.shape[1]
-    stations, fields = coef_ref.shape[1:3]
-    chunks = fbuf.shape[1]
-    copies = fetch([f_hbm.at[n] for n in range(2 * ex)], [fbuf.at[n] for n in range(2 * ex)], in_sem)
-    for copy in copies:
-        copy.wait()
-
-    def put(n, i, value):
-        rows = pl.ds(i, fields, stride=stations)
+    copies = []
+    for e in range(ex):
         for q in range(chunks):
-            obuf[n, q, rows, :] = value[:, q * LANES:(q + 1) * LANES]
-
-    def step(i, carry):
-        xr, xi = carry
-        cr = coef_ref[0, i]
-        ci = coef_ref[1, i]
-        sc = coef_ref[2, i]
-        nxr, nxi = [], []
-        for e in range(ex):
-            fr = station(fbuf.at[e], i, fields, stations)
-            fi = station(fbuf.at[ex + e], i, fields, stations)
-            r = cr * xr[e] - ci * xi[e] + sc * fr
-            m = cr * xi[e] + ci * xr[e] + sc * fi
-            put(e, i, r)
-            put(ex + e, i, m)
-            nxr.append(r)
-            nxi.append(m)
-        return tuple(nxr), tuple(nxi)
-
-    init = (tuple(x0_ref[0, e] for e in range(ex)), tuple(x0_ref[1, e] for e in range(ex)))
-    lax.fori_loop(0, stations, step, init, unroll=4)
-    copies = []
-    for n in range(2 * ex):
-        for q in range(chunks):
-            copy = pltpu.make_async_copy(
-                obuf.at[n, q], out_hbm.at[n, :, pl.ds(q * LANES, LANES)], out_sem.at[n * chunks + q]
-            )
-            copy.start()
-            copies.append(copy)
+            lanes = pl.ds(q * LANES, LANES)
+            for f in range(fields):
+                rows = pl.ds(f * stations, stations)
+                xr = x0_ref[0, e, pl.ds(f, 1), lanes]
+                xi = x0_ref[1, e, pl.ds(f, 1), lanes]
+                gr = gbuf[0, q, rows, :]
+                gi = gbuf[1, q, rows, :]
+                qbuf[e, q, rows, :] = qbuf[e, q, rows, :] + (gr * xr - gi * xi)
+                qbuf[ex + e, q, rows, :] = qbuf[ex + e, q, rows, :] + (gr * xi + gi * xr)
+            for n in (e, ex + e):
+                copy = pltpu.make_async_copy(
+                    qbuf.at[n, q], out_hbm.at[n, :, lanes], out_sem.at[n * chunks + q]
+                )
+                copy.start()
+                copies.append(copy)
     for copy in copies:
         copy.wait()
 
@@ -244,19 +253,21 @@
     chunks = wall // LANES
     slab = (fields * stations, LANES)
     fbuf = pltpu.VMEM((two * ex, chunks) + slab, jnp.float32)
-    coef, x0 = pl.pallas_call(
-        functools.partial(map_kernel, count, subs),
-        out_shape=(
-            jax.ShapeDtypeStruct((3, stations, fields, wall), jnp.float32),
-            jax.ShapeDtypeStruct((2, ex, fields, wall), jnp.float32),
-        ),
+    out_t = pl.pallas_call(
+        functools.partial(resolvent_kernel, count, subs),
+        out_shape=jax.ShapeDtypeStruct(forcing_t.shape, jnp.float32),
         in_specs=[hbm] * 3,
-        out_specs=(vmem, vmem),
+        out_specs=hbm,
         scratch_shapes=[
             pltpu.VMEM((chunks,) + slab, jnp.float32),
             pltpu.VMEM((chunks,) + slab, jnp.float32),
             fbuf,
             pltpu.SemaphoreType.DMA(((2 + two * ex) * chunks,)),
+            pltpu.VMEM((3, stations, fields, wall), jnp.float32),
+            pltpu.VMEM((2, ex, fields, wall), jnp.float32),
+            fbuf,
+            pltpu.VMEM((2, chunks) + slab, jnp.float32),
+            pltpu.SemaphoreType.DMA((two * ex * chunks,)),
             pltpu.VMEM((fields, wall), jnp.float32),
             pltpu.VMEM(packed, jnp.float32),
             pltpu.VMEM((n_slots,) + packed, jnp.float32),
@@ -266,18 +277,6 @@
         ],
         compiler_params=pltpu.CompilerParams(collective_id=0, has_side_effects=True),
     )(rate_t, phase_t, forcing_t)
-    out_t = pl.pallas_call(
-        march_kernel,
-        out_shape=jax.ShapeDtypeStruct(forcing_t.shape, jnp.float32),
-        in_specs=[vmem, hbm, vmem],
-        out_specs=hbm,
-        scratch_shapes=[
-            fbuf,
-            fbuf,
-            pltpu.SemaphoreType.DMA((two * ex * chunks,)),
-            pltpu.SemaphoreType.DMA((two * ex * chunks,)),
-        ],
-    )(coef, forcing_t, x0)
     return jnp.transpose(out_t.reshape(two, ex, fields, stations, wall), (0, 1, 3, 2, 4))
 
 

time: 49.8 us -> 46.1 us (0.926)
  Pallas kernels: 49.5 us -> 43 us
  local copies, waits for them, and re-layouts: 0 us -> 2.97 us
    pallas_call x2 -> x1, Pallas kernels: 49.5 us -> 43 us  [local(): pl.pallas_call(functools.partial(resolvent_kernel, count, subs), out_shap...]
    unnamed x0 -> x1, local copies, waits for them, and re-layouts: none -> 2.97 us
where the time goes in v5:
time: 46.1 us; the launch traced here: 45.9 us
  Pallas kernels  43 us (93%)
  local copies, waits for them, and re-layouts  2.97 us (6%)
    pallas_call x1, Pallas kernels, local(): pl.pallas_call(functools.partial(resolvent_kernel, count, subs), out_shap...  43 us
    unnamed x1, local copies, waits for them, and re-layouts  2.97 us

profile of v5, /device:TPU:1, one launch (start us, length us, event | category | flops | bytes accessed | tf_op | source)
XLA Modules:
  0.0 45.9 jit_solution(14564765116356828794)
XLA Ops:
  0.0 43.0 %shard_map.37 = f32[8,160,384]{2,1,0:T(8,128)} custom-call(f32[160,384]{1,0:T(8,128)} %bitcast.14, f32[160,384]{1,0:T(8,128)} %bitcast.15, f32[8,160,384]{2,1,0:T(8,128)} %bitcast.13), custom_call_target="tpu_custom_call" | custom-call | tf_op jit(solution)/shard_map/pallas_call | solution.py:256
  43.0 3.0 %copy.5 = f32[2,4,32,5,384]{4,2,3,1,0:T(8,128)} copy(f32[2,4,32,5,384]{4,2,3,1,0:T(8,128)} %bitcast.12) | data formatting | bytes 3932160

commit v6 on v5

--- a/solution.py
+++ b/solution.py
@@ -53,8 +53,8 @@
     return jnp.concatenate([buf[q, rows, :] for q in range(buf.shape[0])], axis=1)
 
 
-def resolvent_kernel(count, subs, rate_hbm, phase_hbm, f_hbm, out_hbm,
-                     rbuf, pbuf, fbuf, in_sem, coef_ref, x0_ref, qbuf, gbuf, out_sem,
+def resolvent_kernel(count, subs, rate_hbm, phase_hbm, f_hbm, out_hbm, x0_ref,
+                     rbuf, pbuf, fbuf, in_sem, coef_ref, qbuf, gbuf, out_sem,
                      tmp, pack, recv, cur, send_sem, recv_sem):
     ex = x0_ref.shape[1]
     stations, fields, wall = coef_ref.shape[1:]
@@ -150,6 +150,16 @@
             return npr, npi, tuple(nxr), tuple(nxi)
 
         lax.fori_loop(0, stations, step, init, unroll=4)
+        sends = []
+        for n in range(2 * ex + 2):
+            for q in range(chunks):
+                src = qbuf.at[n, q] if n < 2 * ex else gbuf.at[n - 2 * ex, q]
+                copy = pltpu.make_async_copy(
+                    src, out_hbm.at[n, :, pl.ds(q * LANES, LANES)], out_sem.at[n * chunks + q]
+                )
+                copy.start()
+                sends.append(copy)
+        return sends
 
     def load(ref):
         return [(ref[0, j], ref[1, j]) for j in range(ex + 1)]
@@ -184,7 +194,7 @@
             copy.start()
             copies.append(copy)
         if k == 0:
-            local_march()
+            stored = local_march()
         for n, (i, copy) in enumerate(zip(mine, copies)):
             copy.wait()
             arrived = load(recv.at[i])
@@ -213,25 +223,39 @@
                         c, e, pl.ds(f * chunks + q, 1), :
                     ]
 
-    copies = []
+    for copy in stored:
+        copy.wait()
+
+
+def response_kernel(qg_hbm, x0_ref, out_hbm, qg, obuf, in_sem, out_sem):
+    ex = x0_ref.shape[1]
+    fields = x0_ref.shape[2]
+    stations = qg.shape[1] // fields
+    blocks = qg.shape[0]
+    fetches = []
+    for n in range(blocks):
+        copy = pltpu.make_async_copy(qg_hbm.at[n], qg.at[n], in_sem.at[n])
+        copy.start()
+        fetches.append(copy)
+    fetches[2 * ex].wait()
+    fetches[2 * ex + 1].wait()
+    sends = []
     for e in range(ex):
-        for q in range(chunks):
-            lanes = pl.ds(q * LANES, LANES)
-            for f in range(fields):
-                rows = pl.ds(f * stations, stations)
-                xr = x0_ref[0, e, pl.ds(f, 1), lanes]
-                xi = x0_ref[1, e, pl.ds(f, 1), lanes]
-                gr = gbuf[0, q, rows, :]
-                gi = gbuf[1, q, rows, :]
-                qbuf[e, q, rows, :] = qbuf[e, q, rows, :] + (gr * xr - gi * xi)
-                qbuf[ex + e, q, rows, :] = qbuf[ex + e, q, rows, :] + (gr * xi + gi * xr)
-            for n in (e, ex + e):
-                copy = pltpu.make_async_copy(
-                    qbuf.at[n, q], out_hbm.at[n, :, lanes], out_sem.at[n * chunks + q]
-                )
-                copy.start()
-                copies.append(copy)
-    for copy in copies:
+        fetches[e].wait()
+        fetches[ex + e].wait()
+        for f in range(fields):
+            rows = pl.ds(f * stations, stations)
+            xr = x0_ref[0, e, pl.ds(f, 1), :]
+            xi = x0_ref[1, e, pl.ds(f, 1), :]
+            gr = qg[2 * ex, rows, :]
+            gi = qg[2 * ex + 1, rows, :]
+            obuf[e, rows, :] = qg[e, rows, :] + (gr * xr - gi * xi)
+            obuf[ex + e, rows, :] = qg[ex + e, rows, :] + (gr * xi + gi * xr)
+        for n in (e, ex + e):
+            copy = pltpu.make_async_copy(obuf.at[n], out_hbm.at[n], out_sem.at[n])
+            copy.start()
+            sends.append(copy)
+    for copy in sends:
         copy.wait()
 
 
@@ -253,21 +277,24 @@
     chunks = wall // LANES
     slab = (fields * stations, LANES)
     fbuf = pltpu.VMEM((two * ex, chunks) + slab, jnp.float32)
-    out_t = pl.pallas_call(
+    blocks = two * ex + 2
+    qg, x0 = pl.pallas_call(
         functools.partial(resolvent_kernel, count, subs),
-        out_shape=jax.ShapeDtypeStruct(forcing_t.shape, jnp.float32),
+        out_shape=(
+            jax.ShapeDtypeStruct((blocks,) + forcing_t.shape[1:], jnp.float32),
+            jax.ShapeDtypeStruct((2, ex, fields, wall), jnp.float32),
+        ),
         in_specs=[hbm] * 3,
-        out_specs=hbm,
+        out_specs=(hbm, vmem),
         scratch_shapes=[
             pltpu.VMEM((chunks,) + slab, jnp.float32),
             pltpu.VMEM((chunks,) + slab, jnp.float32),
             fbuf,
             pltpu.SemaphoreType.DMA(((2 + two * ex) * chunks,)),
             pltpu.VMEM((3, stations, fields, wall), jnp.float32),
-            pltpu.VMEM((2, ex, fields, wall), jnp.float32),
             fbuf,
             pltpu.VMEM((2, chunks) + slab, jnp.float32),
-            pltpu.SemaphoreType.DMA((two * ex * chunks,)),
+            pltpu.SemaphoreType.DMA((blocks * chunks,)),
             pltpu.VMEM((fields, wall), jnp.float32),
             pltpu.VMEM(packed, jnp.float32),
             pltpu.VMEM((n_slots,) + packed, jnp.float32),
@@ -277,6 +304,18 @@
         ],
         compiler_params=pltpu.CompilerParams(collective_id=0, has_side_effects=True),
     )(rate_t, phase_t, forcing_t)
+    out_t = pl.pallas_call(
+        response_kernel,
+        out_shape=jax.ShapeDtypeStruct(forcing_t.shape, jnp.float32),
+        in_specs=[hbm, vmem],
+        out_specs=hbm,
+        scratch_shapes=[
+            pltpu.VMEM(qg.shape, jnp.float32),
+            pltpu.VMEM(forcing_t.shape, jnp.float32),
+            pltpu.SemaphoreType.DMA((blocks,)),
+            pltpu.SemaphoreType.DMA((two * ex,)),
+        ],
+    )(qg, x0)
     return jnp.transpose(out_t.reshape(two, ex, fields, stations, wall), (0, 1, 3, 2, 4))
 
 

time: 46.1 us -> 46.7 us (1.013)
  Pallas kernels: 43 us -> 46.5 us
  local copies, waits for them, and re-layouts: 2.97 us -> 0 us
    pallas_call x0 -> x1, Pallas kernels: none -> 4.13 us  [local(): pl.pallas_call(response_kernel, out_shape=jax.ShapeDtypeStruct(forcing_t....]
    unnamed x1 -> x0, local copies, waits for them, and re-layouts: 2.97 us -> none
    pallas_call x1, Pallas kernels: 43 us -> 42.4 us  [local(): pl.pallas_call(functools.partial(resolvent_kernel, count, subs), out_shap...]
where the time goes in v6:
time: 46.7 us; the launch traced here: 46.5 us
  Pallas kernels  46.5 us (100%)
    pallas_call x1, Pallas kernels, local(): pl.pallas_call(functools.partial(resolvent_kernel, count, subs), out_shap...  42.4 us
    pallas_call x1, Pallas kernels, local(): pl.pallas_call(response_kernel, out_shape=jax.ShapeDtypeStruct(forcing_t....  4.13 us

profile of v6, /device:TPU:1, one launch (start us, length us, event | category | flops | bytes accessed | tf_op | source)
XLA Modules:
  0.0 46.5 jit_solution(2239617097199573576)
XLA Ops:
  0.0 42.4 %shard_map.37 = (f32[10,160,384]{2,1,0:T(8,128)}, f32[2,4,5,384]{3,2,1,0:T(8,128)}) custom-call(f32[160,384]{1,0:T(8,128)} %bitcast.13, f32[160,384]{1,0:T(8,128)} %bitcast.14, f32[8,160,384]{2,1,0:T(8,128)} %bitcast.12), custom_call_target="tpu_custom_call" | custom-call | tf_op jit(solution)/shard_map/pallas_call | solution.py:281
  42.4 4.1 %shard_map.38 = f32[8,160,384]{2,1,0:T(8,128)} custom-call(f32[10,160,384]{2,1,0:T(8,128)} %get-tuple-element.7.qg_hbm, f32[2,4,5,384]{3,2,1,0:T(8,128)} %get-tuple-element.8.x0_ref), custom_call_target="tpu_custom_call" | custom-call | tf_op jit(solution)/shard_map/pallas_call | solution.py:307

commit v7 on v5

--- a/solution.py
+++ b/solution.py
@@ -53,8 +53,8 @@
     return jnp.concatenate([buf[q, rows, :] for q in range(buf.shape[0])], axis=1)
 
 
-def resolvent_kernel(count, subs, rate_hbm, phase_hbm, f_hbm, out_hbm,
-                     rbuf, pbuf, fbuf, in_sem, coef_ref, x0_ref, qbuf, gbuf, out_sem,
+def resolvent_kernel(count, subs, rate_hbm, phase_hbm, f_hbm, out_hbm, gr_hbm, gi_hbm, x0_ref,
+                     rbuf, pbuf, fbuf, in_sem, coef_ref, qbuf, gbuf, out_sem,
                      tmp, pack, recv, cur, send_sem, recv_sem):
     ex = x0_ref.shape[1]
     stations, fields, wall = coef_ref.shape[1:]
@@ -150,6 +150,18 @@
             return npr, npi, tuple(nxr), tuple(nxi)
 
         lax.fori_loop(0, stations, step, init, unroll=4)
+        sends = []
+        for n in range(2 * ex + 2):
+            for q in range(chunks):
+                lanes = pl.ds(q * LANES, LANES)
+                if n < 2 * ex:
+                    src, dst = qbuf.at[n, q], out_hbm.at[n, :, lanes]
+                else:
+                    src, dst = gbuf.at[n - 2 * ex, q], (gr_hbm, gi_hbm)[n - 2 * ex].at[:, lanes]
+                copy = pltpu.make_async_copy(src, dst, out_sem.at[n * chunks + q])
+                copy.start()
+                sends.append(copy)
+        return sends
 
     def load(ref):
         return [(ref[0, j], ref[1, j]) for j in range(ex + 1)]
@@ -184,7 +196,7 @@
             copy.start()
             copies.append(copy)
         if k == 0:
-            local_march()
+            stored = local_march()
         for n, (i, copy) in enumerate(zip(mine, copies)):
             copy.wait()
             arrived = load(recv.at[i])
@@ -212,26 +224,10 @@
                     x0_ref[c, e, pl.ds(f, 1), pl.ds(q * LANES, LANES)] = ent[
                         c, e, pl.ds(f * chunks + q, 1), :
                     ]
-
-    copies = []
-    for e in range(ex):
-        for q in range(chunks):
-            lanes = pl.ds(q * LANES, LANES)
-            for f in range(fields):
-                rows = pl.ds(f * stations, stations)
-                xr = x0_ref[0, e, pl.ds(f, 1), lanes]
-                xi = x0_ref[1, e, pl.ds(f, 1), lanes]
-                gr = gbuf[0, q, rows, :]
-                gi = gbuf[1, q, rows, :]
-                qbuf[e, q, rows, :] = qbuf[e, q, rows, :] + (gr * xr - gi * xi)
-                qbuf[ex + e, q, rows, :] = qbuf[ex + e, q, rows, :] + (gr * xi + gi * xr)
-            for n in (e, ex + e):
-                copy = pltpu.make_async_copy(
-                    qbuf.at[n, q], out_hbm.at[n, :, lanes], out_sem.at[n * chunks + q]
-                )
-                copy.start()
-                copies.append(copy)
-    for copy in copies:
+    x0_ref[2] = -x0_ref[1]
+    x0_ref[3] = x0_ref[0]
+
+    for copy in stored:
         copy.wait()
 
 
@@ -253,21 +249,26 @@
     chunks = wall // LANES
     slab = (fields * stations, LANES)
     fbuf = pltpu.VMEM((two * ex, chunks) + slab, jnp.float32)
-    out_t = pl.pallas_call(
+    blocks = two * ex + 2
+    offset, gain_r, gain_i, x0 = pl.pallas_call(
         functools.partial(resolvent_kernel, count, subs),
-        out_shape=jax.ShapeDtypeStruct(forcing_t.shape, jnp.float32),
+        out_shape=(
+            jax.ShapeDtypeStruct(forcing_t.shape, jnp.float32),
+            jax.ShapeDtypeStruct(forcing_t.shape[1:], jnp.float32),
+            jax.ShapeDtypeStruct(forcing_t.shape[1:], jnp.float32),
+            jax.ShapeDtypeStruct((4, ex, fields, wall), jnp.float32),
+        ),
         in_specs=[hbm] * 3,
-        out_specs=hbm,
+        out_specs=(hbm, hbm, hbm, vmem),
         scratch_shapes=[
             pltpu.VMEM((chunks,) + slab, jnp.float32),
             pltpu.VMEM((chunks,) + slab, jnp.float32),
             fbuf,
             pltpu.SemaphoreType.DMA(((2 + two * ex) * chunks,)),
             pltpu.VMEM((3, stations, fields, wall), jnp.float32),
-            pltpu.VMEM((2, ex, fields, wall), jnp.float32),
             fbuf,
             pltpu.VMEM((2, chunks) + slab, jnp.float32),
-            pltpu.SemaphoreType.DMA((two * ex * chunks,)),
+            pltpu.SemaphoreType.DMA((blocks * chunks,)),
             pltpu.VMEM((fields, wall), jnp.float32),
             pltpu.VMEM(packed, jnp.float32),
             pltpu.VMEM((n_slots,) + packed, jnp.float32),
@@ -277,7 +278,13 @@
         ],
         compiler_params=pltpu.CompilerParams(collective_id=0, has_side_effects=True),
     )(rate_t, phase_t, forcing_t)
-    return jnp.transpose(out_t.reshape(two, ex, fields, stations, wall), (0, 1, 3, 2, 4))
+    x0 = x0.reshape(2, 2, ex, fields, 1, wall)
+    out_t = (
+        offset.reshape(two, ex, fields, stations, wall)
+        + gain_r.reshape(fields, stations, wall) * x0[0]
+        + gain_i.reshape(fields, stations, wall) * x0[1]
+    )
+    return jnp.transpose(out_t, (0, 1, 3, 2, 4))
 
 
 def solution(mesh):

time: 46.1 us -> 47 us (1.020)
  other arithmetic: 0 us -> 3.4 us
  local copies, waits for them, and re-layouts: 2.97 us -> 0.96 us
  Pallas kernels: 43 us -> 42.4 us
    transpose x0 -> x1, other arithmetic: none -> 3.4 us  [local(): return jnp.transpose(out_t, (0, 1, 3, 2, 4))]
    unnamed x1 -> x0, local copies, waits for them, and re-layouts: 2.97 us -> none
    slice x0 -> x1, local copies, waits for them, and re-layouts: none -> 0.96 us  [local(): x0[0]]
    pallas_call x1, Pallas kernels: 43 us -> 42.4 us  [local(): pl.pallas_call(functools.partial(resolvent_kernel, count, subs), out_shap...]
where the time goes in v7:
time: 47 us; the launch traced here: 46.8 us
  Pallas kernels  42.4 us (90%)
  other arithmetic  3.4 us (7%)
  local copies, waits for them, and re-layouts  0.96 us (2%)
    pallas_call x1, Pallas kernels, local(): pl.pallas_call(functools.partial(resolvent_kernel, count, subs), out_shap...  42.4 us
    transpose x1, other arithmetic, local(): return jnp.transpose(out_t, (0, 1, 3, 2, 4))  3.4 us
    slice x1, local copies, waits for them, and re-layouts, local(): x0[0]  0.96 us

profile of v7, /device:TPU:1, one launch (start us, length us, event | category | flops | bytes accessed | tf_op | source)
XLA Modules:
  0.0 46.8 jit_solution(7230362708898615831)
XLA Ops:
  0.0 42.4 %shard_map.37 = (f32[8,160,384]{2,1,0:T(8,128)}, f32[160,384]{1,0:T(8,128)}, f32[160,384]{1,0:T(8,128)}, f32[4,4,5,384]{3,2,1,0:T(8,128)}) custom-call(f32[160,384]{1,0:T(8,128)} %bitcast.16, f32[160,384]{1,0:T(8,128)} %bitcast.17, f32[8,160,384]{2,1,0:T(8,128)} %bitcast.14), custom_call_target="tpu_custom_call" | custom-call | tf_op jit(solution)/shard_map/pallas_call | solution.py:253
  42.4 1.0 %fusion = (f32[2,4,5,384]{3,2,1,0:T(8,128)S(1)}, f32[2,4,5,384]{3,2,1,0:T(8,128)S(1)}) fusion(f32[4,4,5,384]{3,2,1,0:T(8,128)} %get-tuple-element.11), kind=kLoop, calls=%fused_computation.1 | loop fusion | bytes 245760 | tf_op jit(solution)/shard_map/slice | solution.py:284
  43.4 3.4 %add_bitcast_fusion = f32[2,4,32,5,384]{4,2,3,1,0:T(8,128)} fusion(f32[2,4,5,32,384]{4,3,2,1,0:T(8,128)} %bitcast.15, f32[2,4,5,384]{3,2,1,0:T(8,128)S(1)} %get-tuple-element.14, f32[5,32,384]{2,1,0:T(8,128)} %bitcast.19, f32[2,4,5,384]{3,2,1,0:T(8,128)S(1)} %get-tuple-element.13, f32[5,32,384]{2,1,0:T(8,128)} %bitcast.18), kind=kLoop, calls=%fused_computation | loop fusion | flops 1966080 | bytes 4546560 | tf_op jit(solution)/shard_map/transpose | solution.py:287

commit v8 on v5

--- a/solution.py
+++ b/solution.py
@@ -57,8 +57,9 @@
                      rbuf, pbuf, fbuf, in_sem, coef_ref, x0_ref, qbuf, gbuf, out_sem,
                      tmp, pack, recv, cur, send_sem, recv_sem):
     ex = x0_ref.shape[1]
-    stations, fields, wall = coef_ref.shape[1:]
+    fields, wall = x0_ref.shape[2:]
     chunks = wall // LANES
+    stations = rbuf.shape[1] // fields
     copies = fetch(
         [rate_hbm, phase_hbm] + [f_hbm.at[n] for n in range(2 * ex)],
         [rbuf, pbuf] + [fbuf.at[n] for n in range(2 * ex)],
@@ -82,18 +83,21 @@
     for copy in copies:
         copy.wait()
 
+    station_of_row = lax.broadcasted_iota(jnp.int32, rbuf.shape[1:], 0) % stations
+    sponge = jnp.where(me * stations + station_of_row >= first_fringe, damp, jnp.float32(1.0))
+    for q in range(chunks):
+        r = rbuf[q]
+        ph = pbuf[q]
+        mag = jnp.exp(-r) * sponge
+        coef_ref[0, q] = mag * jnp.cos(ph)
+        coef_ref[1, q] = mag * jnp.sin(ph)
+        coef_ref[2, q] = jnp.sqrt(-expm1(-2.0 * r))
+
     def step(i, carry):
         pr, pi, xr, xi = carry
-        r = station(rbuf, i, fields, stations)
-        ph = station(pbuf, i, fields, stations)
-        sponge = jnp.where(me * stations + i >= first_fringe, damp, jnp.float32(1.0))
-        mag = jnp.exp(-r) * sponge
-        cr = mag * jnp.cos(ph)
-        ci = mag * jnp.sin(ph)
-        sc = jnp.sqrt(-expm1(-2.0 * r))
-        coef_ref[0, i] = cr
-        coef_ref[1, i] = ci
-        coef_ref[2, i] = sc
+        cr = station(coef_ref.at[0], i, fields, stations)
+        ci = station(coef_ref.at[1], i, fields, stations)
+        sc = station(coef_ref.at[2], i, fields, stations)
         npr = cr * pr - ci * pi
         npi = cr * pi + ci * pr
         nxr, nxi = [], []
@@ -130,9 +134,9 @@
     def local_march():
         def step(i, carry):
             pr, pi, xr, xi = carry
-            cr = coef_ref[0, i]
-            ci = coef_ref[1, i]
-            sc = coef_ref[2, i]
+            cr = station(coef_ref.at[0], i, fields, stations)
+            ci = station(coef_ref.at[1], i, fields, stations)
+            sc = station(coef_ref.at[2], i, fields, stations)
             npr = cr * pr - ci * pi
             npi = cr * pi + ci * pr
             put(gbuf, 0, i, npr)
@@ -263,7 +267,7 @@
             pltpu.VMEM((chunks,) + slab, jnp.float32),
             fbuf,
             pltpu.SemaphoreType.DMA(((2 + two * ex) * chunks,)),
-            pltpu.VMEM((3, stations, fields, wall), jnp.float32),
+            pltpu.VMEM((3, chunks) + slab, jnp.float32),
             pltpu.VMEM((2, ex, fields, wall), jnp.float32),
             fbuf,
             pltpu.VMEM((2, chunks) + slab, jnp.float32),

time: 46.1 us -> 47.4 us (1.028)
  Pallas kernels: 43 us -> 44.2 us
    pallas_call x1, Pallas kernels: 43 us -> 44.2 us  [local(): pl.pallas_call(functools.partial(resolvent_kernel, count, subs), out_shap...]
where the time goes in v8:
time: 47.4 us; the launch traced here: 47.2 us
  Pallas kernels  44.2 us (93%)
  local copies, waits for them, and re-layouts  2.97 us (6%)
    pallas_call x1, Pallas kernels, local(): pl.pallas_call(functools.partial(resolvent_kernel, count, subs), out_shap...  44.2 us
    unnamed x1, local copies, waits for them, and re-layouts  2.97 us

profile of v8, /device:TPU:1, one launch (start us, length us, event | category | flops | bytes accessed | tf_op | source)
XLA Modules:
  0.0 47.2 jit_solution(8600297072731227144)
XLA Ops:
  0.0 44.2 %shard_map.37 = f32[8,160,384]{2,1,0:T(8,128)} custom-call(f32[160,384]{1,0:T(8,128)} %bitcast.14, f32[160,384]{1,0:T(8,128)} %bitcast.15, f32[8,160,384]{2,1,0:T(8,128)} %bitcast.13), custom_call_target="tpu_custom_call" | custom-call | tf_op jit(solution)/shard_map/pallas_call | solution.py:260
  44.2 3.0 %copy.5 = f32[2,4,32,5,384]{4,2,3,1,0:T(8,128)} copy(f32[2,4,32,5,384]{4,2,3,1,0:T(8,128)} %bitcast.12) | data formatting | bytes 3932160

commit v9 on v5

--- a/solution.py
+++ b/solution.py
@@ -108,7 +108,7 @@
     one = jnp.ones(shape, jnp.float32)
     zero = jnp.zeros(shape, jnp.float32)
     init = (one, zero, (zero,) * ex, (zero,) * ex)
-    pr, pi, xr, xi = lax.fori_loop(0, stations, step, init, unroll=4)
+    pr, pi, xr, xi = lax.fori_loop(0, stations, step, init, unroll=8)
 
     values = [(xr[e], xi[e]) for e in range(ex)] + [(pr, pi)]
     for j, pair in enumerate(values):

time: 46.1 us -> 46.1 us (level)
  no operation moved by 1% of the time
where the time goes in v9:
time: 46.1 us; the launch traced here: 45.8 us
  Pallas kernels  42.9 us (93%)
  local copies, waits for them, and re-layouts  2.97 us (6%)
    pallas_call x1, Pallas kernels, local(): pl.pallas_call(functools.partial(resolvent_kernel, count, subs), out_shap...  42.9 us
    unnamed x1, local copies, waits for them, and re-layouts  2.97 us

profile of v9, /device:TPU:1, one launch (start us, length us, event | category | flops | bytes accessed | tf_op | source)
XLA Modules:
  0.0 45.8 jit_solution(8418875661546420812)
XLA Ops:
  0.0 42.9 %shard_map.37 = f32[8,160,384]{2,1,0:T(8,128)} custom-call(f32[160,384]{1,0:T(8,128)} %bitcast.14, f32[160,384]{1,0:T(8,128)} %bitcast.15, f32[8,160,384]{2,1,0:T(8,128)} %bitcast.13), custom_call_target="tpu_custom_call" | custom-call | tf_op jit(solution)/shard_map/pallas_call | solution.py:256
  42.9 3.0 %copy.5 = f32[2,4,32,5,384]{4,2,3,1,0:T(8,128)} copy(f32[2,4,32,5,384]{4,2,3,1,0:T(8,128)} %bitcast.12) | data formatting | bytes 3932160

commit v10 on v5

--- a/solution.py
+++ b/solution.py
@@ -110,13 +110,18 @@
     init = (one, zero, (zero,) * ex, (zero,) * ex)
     pr, pi, xr, xi = lax.fori_loop(0, stations, step, init, unroll=4)
 
+    rows_per = fields * chunks
+
+    def block(c, j):
+        return pl.ds((c * (ex + 1) + j) * rows_per, rows_per)
+
     values = [(xr[e], xi[e]) for e in range(ex)] + [(pr, pi)]
     for j, pair in enumerate(values):
         for c in range(2):
             tmp[...] = pair[c]
             for f in range(fields):
                 for q in range(chunks):
-                    pack[c, j, pl.ds(f * chunks + q, 1), :] = tmp[
+                    pack[pl.ds((c * (ex + 1) + j) * rows_per + f * chunks + q, 1), :] = tmp[
                         pl.ds(f, 1), pl.ds(q * LANES, LANES)
                     ]
 
@@ -152,7 +157,7 @@
         lax.fori_loop(0, stations, step, init, unroll=4)
 
     def load(ref):
-        return [(ref[0, j], ref[1, j]) for j in range(ex + 1)]
+        return [(ref[block(0, j), :], ref[block(1, j), :]) for j in range(ex + 1)]
 
     def compose(earlier, later):
         ar, ai = later[ex]
@@ -192,8 +197,8 @@
         if k + 1 < len(rounds):
             dst = cur.at[k + 1]
             for j, (nr, ni) in enumerate(held):
-                dst[0, j] = nr
-                dst[1, j] = ni
+                dst[block(0, j), :] = nr
+                dst[block(1, j), :] = ni
             held = load(dst)
 
     gr, gi = held[ex]
@@ -203,14 +208,14 @@
     ent = cur.at[0]
     for j in range(ex):
         br, bi = held[j]
-        ent[0, j] = (br * denom_re + bi * denom_im) / size
-        ent[1, j] = (bi * denom_re - br * denom_im) / size
+        ent[block(0, j), :] = (br * denom_re + bi * denom_im) / size
+        ent[block(1, j), :] = (bi * denom_re - br * denom_im) / size
     for c in range(2):
         for e in range(ex):
             for f in range(fields):
                 for q in range(chunks):
                     x0_ref[c, e, pl.ds(f, 1), pl.ds(q * LANES, LANES)] = ent[
-                        c, e, pl.ds(f * chunks + q, 1), :
+                        pl.ds((c * (ex + 1) + e) * rows_per + f * chunks + q, 1), :
                     ]
 
     copies = []
@@ -247,7 +252,7 @@
     )
     n_slots = len(slots_of(count))
     n_rounds = len(rounds_of(count))
-    packed = (2, ex + 1, fields * wall // LANES, LANES)
+    packed = (2 * (ex + 1) * fields * wall // LANES, LANES)
     vmem = pl.BlockSpec(memory_space=pltpu.VMEM)
     hbm = pl.BlockSpec(memory_space=pl.ANY)
     chunks = wall // LANES

time: 46.1 us -> 46.1 us (level)
  no operation moved by 1% of the time
where the time goes in v10:
time: 46.1 us; the launch traced here: 46 us
  Pallas kernels  43 us (93%)
  local copies, waits for them, and re-layouts  2.97 us (6%)
    pallas_call x1, Pallas kernels, local(): pl.pallas_call(functools.partial(resolvent_kernel, count, subs), out_shap...  43 us
    unnamed x1, local copies, waits for them, and re-layouts  2.97 us

profile of v10, /device:TPU:1, one launch (start us, length us, event | category | flops | bytes accessed | tf_op | source)
XLA Modules:
  0.0 46.0 jit_solution(14914049509715742838)
XLA Ops:
  0.0 43.0 %shard_map.37 = f32[8,160,384]{2,1,0:T(8,128)} custom-call(f32[160,384]{1,0:T(8,128)} %bitcast.14, f32[160,384]{1,0:T(8,128)} %bitcast.15, f32[8,160,384]{2,1,0:T(8,128)} %bitcast.13), custom_call_target="tpu_custom_call" | custom-call | tf_op jit(solution)/shard_map/pallas_call | solution.py:261
  43.0 3.0 %copy.5 = f32[2,4,32,5,384]{4,2,3,1,0:T(8,128)} copy(f32[2,4,32,5,384]{4,2,3,1,0:T(8,128)} %bitcast.12) | data formatting | bytes 3932160

commit v11 on v5

--- a/solution.py
+++ b/solution.py
@@ -127,7 +127,7 @@
         for q in range(chunks):
             buf[n, q, rows, :] = value[:, q * LANES:(q + 1) * LANES]
 
-    def local_march():
+    def local_march(lo, hi, carry):
         def step(i, carry):
             pr, pi, xr, xi = carry
             cr = coef_ref[0, i]
@@ -149,7 +149,7 @@
                 nxi.append(m)
             return npr, npi, tuple(nxr), tuple(nxi)
 
-        lax.fori_loop(0, stations, step, init, unroll=4)
+        return lax.fori_loop(lo, hi, step, carry, unroll=4)
 
     def load(ref):
         return [(ref[0, j], ref[1, j]) for j in range(ex + 1)]
@@ -184,7 +184,9 @@
             copy.start()
             copies.append(copy)
         if k == 0:
-            local_march()
+            marched = local_march(0, stations // 2, init)
+        if k == 1:
+            local_march(stations // 2, stations, marched)
         for n, (i, copy) in enumerate(zip(mine, copies)):
             copy.wait()
             arrived = load(recv.at[i])

time: 46.1 us -> 46.1 us (level)
  no operation moved by 1% of the time
where the time goes in v11:
time: 46.1 us; the launch traced here: 45.9 us
  Pallas kernels  43 us (93%)
  local copies, waits for them, and re-layouts  2.97 us (6%)
    pallas_call x1, Pallas kernels, local(): pl.pallas_call(functools.partial(resolvent_kernel, count, subs), out_shap...  43 us
    unnamed x1, local copies, waits for them, and re-layouts  2.97 us

profile of v11, /device:TPU:1, one launch (start us, length us, event | category | flops | bytes accessed | tf_op | source)
XLA Modules:
  0.0 45.9 jit_solution(4436560891000913989)
XLA Ops:
  0.0 43.0 %shard_map.37 = f32[8,160,384]{2,1,0:T(8,128)} custom-call(f32[160,384]{1,0:T(8,128)} %bitcast.14, f32[160,384]{1,0:T(8,128)} %bitcast.15, f32[8,160,384]{2,1,0:T(8,128)} %bitcast.13), custom_call_target="tpu_custom_call" | custom-call | tf_op jit(solution)/shard_map/pallas_call | solution.py:258
  43.0 3.0 %copy.5 = f32[2,4,32,5,384]{4,2,3,1,0:T(8,128)} copy(f32[2,4,32,5,384]{4,2,3,1,0:T(8,128)} %bitcast.12) | data formatting | bytes 3932160

commit v12 on v11

--- a/solution.py
+++ b/solution.py
@@ -207,13 +207,6 @@
         br, bi = held[j]
         ent[0, j] = (br * denom_re + bi * denom_im) / size
         ent[1, j] = (bi * denom_re - br * denom_im) / size
-    for c in range(2):
-        for e in range(ex):
-            for f in range(fields):
-                for q in range(chunks):
-                    x0_ref[c, e, pl.ds(f, 1), pl.ds(q * LANES, LANES)] = ent[
-                        c, e, pl.ds(f * chunks + q, 1), :
-                    ]
 
     copies = []
     for e in range(ex):
@@ -221,8 +214,8 @@
             lanes = pl.ds(q * LANES, LANES)
             for f in range(fields):
                 rows = pl.ds(f * stations, stations)
-                xr = x0_ref[0, e, pl.ds(f, 1), lanes]
-                xi = x0_ref[1, e, pl.ds(f, 1), lanes]
+                xr = ent[0, e, pl.ds(f * chunks + q, 1), :]
+                xi = ent[1, e, pl.ds(f * chunks + q, 1), :]
                 gr = gbuf[0, q, rows, :]
                 gi = gbuf[1, q, rows, :]
                 qbuf[e, q, rows, :] = qbuf[e, q, rows, :] + (gr * xr - gi * xi)

time: 46.1 us -> 46.1 us (level)
  no operation moved by 1% of the time
where the time goes in v12:
time: 46.1 us; the launch traced here: 45.9 us
  Pallas kernels  42.9 us (93%)
  local copies, waits for them, and re-layouts  2.97 us (6%)
    pallas_call x1, Pallas kernels, local(): pl.pallas_call(functools.partial(resolvent_kernel, count, subs), out_shap...  42.9 us
    unnamed x1, local copies, waits for them, and re-layouts  2.97 us

profile of v12, /device:TPU:1, one launch (start us, length us, event | category | flops | bytes accessed | tf_op | source)
XLA Modules:
  0.0 45.9 jit_solution(9053985744613533396)
XLA Ops:
  0.0 42.9 %shard_map.37 = f32[8,160,384]{2,1,0:T(8,128)} custom-call(f32[160,384]{1,0:T(8,128)} %bitcast.14, f32[160,384]{1,0:T(8,128)} %bitcast.15, f32[8,160,384]{2,1,0:T(8,128)} %bitcast.13), custom_call_target="tpu_custom_call" | custom-call | tf_op jit(solution)/shard_map/pallas_call | solution.py:251
  42.9 3.0 %copy.5 = f32[2,4,32,5,384]{4,2,3,1,0:T(8,128)} copy(f32[2,4,32,5,384]{4,2,3,1,0:T(8,128)} %bitcast.12) | data formatting | bytes 3932160
